TPU v7x, 256 devices: a whole 4x4x8 slice. The times are simulated.
256 devices in a mesh: order: 32 (over x, y, core), axial: 8 (over z).
Axes of the slice: x: 4, y: 4, z: 8, core: 2. Of those that a mesh axis runs over, the one named last changes fastest.
Arguments:
- coefficients: bfloat16 [4, 2, 1024, 16, 1024], P(None, None, 'order', 'axial'), may hold values from -0.005859375 to 0.005859375
- order_lists: int32 [1024], replicated, may hold values from 0 to 1023, as said below
- lengths: int32 [1024], replicated, may hold values from 128 to 1024, as said below
Outputs:
- advection: bfloat16 [3, 2, 1024, 16, 1024], P(None, None, 'order', 'axial')
Inputs may be any that keep to these rules, and one draw needn't show every extreme that they name: `order_lists`: a permutation of the orders 0 to 1023; the device with index j along order holds slots j * 32 to (j + 1) * 32 - 1 of coefficients and advection. lengths[m] minus (128 + ((1023 - m) * 768) // 1023) lies in 0 to 128.
All inputs are finite; a program needn't handle non-finite values.
Results may differ from a plain program's by a relative error of at most 0.0095.
Values may be sent and summed in bfloat16 or wider, within the bound.
No kernel may reach another device: no remote copies, remote signals or barrier semaphores. Data moves between devices by JAX's collectives and lax.ppermute only.
A program may use at most 128 MiB of HBM per device.

v0:
```python
import functools
import math

import jax
import jax.numpy as jnp
import numpy as np
from jax import lax
from jax.experimental import pallas as pl
from jax.experimental.pallas import tpu as pltpu
from jax.sharding import PartitionSpec as P

R = 1024
F32 = jnp.float32
BF16 = jnp.bfloat16


def radial_constants(radius_count, mode_count):
    radius_ids = np.arange(radius_count)
    mode_ids = np.arange(mode_count)
    phases = mode_ids[None, :] * (2 * radius_ids[:, None] + 1) % (4 * radius_count)
    cosines = np.cos(phases * (math.pi / (2 * radius_count))).astype(np.float32)
    synthesis = cosines.astype(jnp.bfloat16)
    analysis = (cosines * np.float32(math.sqrt(2.0 / radius_count))).astype(jnp.bfloat16)
    return synthesis, analysis


def plane_matrices(slots):
    width = 2 * slots * 2
    pair = width // 2
    inner = np.arange(width)
    plane, rest = inner % 2, inner // 2
    gather = np.zeros((width, width), np.float32)
    gather[inner, plane * pair + rest] = 1.0
    eye = np.eye(pair, dtype=np.float32)
    own = np.kron(eye, np.array([[0, 8], [-8, 0]], np.float32))
    low = np.kron(eye, np.array([[1, -8], [0, 1]], np.float32))
    high = np.kron(eye, np.array([[-1, 0], [8, -1]], np.float32))
    rows = np.concatenate([own, low, high], axis=1)
    swap = np.roll(np.eye(width, dtype=np.float32), pair, axis=1)
    both = np.concatenate([gather, gather @ swap], axis=1)
    slope = rows.T @ both
    return (
        rows.astype(jnp.bfloat16),
        both.astype(jnp.bfloat16),
        slope.astype(jnp.bfloat16),
        gather.T.astype(jnp.bfloat16),
    )


def dot(a, b, dims):
    return lax.dot_general(a, b, (dims, ((), ())), preferred_element_type=F32)


HERE = pl.BlockSpec(memory_space=pltpu.VMEM)
FAR = pl.BlockSpec(memory_space=pltpu.HBM)
SCALARS = pl.BlockSpec(memory_space=pltpu.SMEM)


def in_hbm(x):
    return pltpu.with_memory_space_constraint(x, pltpu.HBM)


def call(kernel, name, out_shape, in_specs, out_specs, scratch=(), limit=16):
    return pl.pallas_call(
        kernel,
        out_shape=out_shape,
        in_specs=in_specs,
        out_specs=out_specs,
        scratch_shapes=list(scratch),
        compiler_params=pltpu.CompilerParams(vmem_limit_bytes=limit << 20),
        name=name,
    )


def stage_kernel(x_ref, slope_ref, raw_ref, sem):
    copies = []
    for field in range(4):
        target = slope_ref if field < 2 else raw_ref
        for part in range(2):
            copies.append(pltpu.make_async_copy(
                x_ref.at[field, part], target.at[field % 2, part], sem.at[2 * field + part]))
    for copy in copies:
        copy.start()
    for copy in copies:
        copy.wait()


def stage(x):
    half = (2,) + x.shape[1:]
    return call(
        stage_kernel, "stage",
        (pltpu.VMEM(half, BF16), pltpu.VMEM(half, BF16)),
        [FAR], (HERE, HERE), [pltpu.SemaphoreType.DMA((8,))],
    )(in_hbm(x))


def field_rows(ref, field):
    block = ref[field]
    return block.reshape(math.prod(block.shape[:-1]), block.shape[-1])


def masked_rows(block, lens, weight):
    modes = lax.broadcasted_iota(jnp.int32, block.shape, 1)
    return jnp.where(modes < lens[:, :1], block.astype(F32) * weight[:, :1], 0.0).astype(BF16)


def send_bands(table_ref, rows, out_ref, buffer, sem, loads=None, count=4):
    size = table_ref.shape[0] // count
    copies = []
    for i in range(count):
        part = pl.ds(i * size, size)
        if loads is not None:
            loads[i].wait()
        buffer[part, :] = dot(table_ref[part, :], rows, ((1,), (1,))).astype(BF16)
        copies.append(pltpu.make_async_copy(buffer.at[part], out_ref.at[part], sem.at[i]))
        copies[-1].start()
    for copy in copies:
        copy.wait()


def raw_kernel(slots, orders_ref, lengths_ref, x_ref, table_ref, out_ref, lens_ref, weight_ref,
               buffer, sem, held_table, load_sem):
    size = held_table.shape[0] // 4
    loads = [
        pltpu.make_async_copy(table_ref.at[pl.ds(i * size, size)],
                              held_table.at[pl.ds(i * size, size)], load_sem.at[i])
        for i in range(4)
    ]
    for load in loads:
        load.start()
    base = lax.axis_index("order") * slots
    rows = 2 * slots
    slot_of = lax.broadcasted_iota(jnp.int32, (rows, 128), 0) // 2
    lens = jnp.zeros((rows, 128), jnp.int32)
    order = jnp.zeros((rows, 128), jnp.int32)
    for slot in range(slots):
        here = orders_ref[base + slot]
        lens = jnp.where(slot_of == slot, lengths_ref[here], lens)
        order = jnp.where(slot_of == slot, here, order)
    lens = jnp.concatenate([lens, lens], axis=0)
    weight = jnp.where(order == 0, 1.0, 2.0).astype(F32)
    weight = jnp.concatenate([weight, weight], axis=0)
    lens_ref[...] = lens
    weight_ref[...] = weight
    held = [masked_rows(field_rows(x_ref, field), lens, weight) for field in range(2)]
    send_bands(held_table, jnp.concatenate(held, axis=0), out_ref, buffer, sem, loads)


def radial_raw(orders, lengths, x, table):
    rows = 2 * math.prod(x.shape[1:-1])
    return call(
        functools.partial(raw_kernel, x.shape[2]), "radial_raw",
        (pltpu.HBM((R, rows), BF16),
         jax.ShapeDtypeStruct((rows // 2, 128), jnp.int32),
         jax.ShapeDtypeStruct((rows // 2, 128), F32)),
        [SCALARS, SCALARS, HERE, FAR], (FAR, HERE, HERE),
        [pltpu.VMEM((R, rows), BF16), pltpu.SemaphoreType.DMA((4,)),
         pltpu.VMEM(table.shape, BF16), pltpu.SemaphoreType.DMA((4,))],
    )(orders, lengths, x, in_hbm(table))


def slope_kernel(x_ref, low_ref, high_ref, lens_ref, weight_ref, rows_ref, table_ref, out_ref,
                 buffer, sem):
    held = []
    for field in range(2):
        stacked = jnp.concatenate(
            [field_rows(x_ref, field), field_rows(low_ref, field), field_rows(high_ref, field)],
            axis=0,
        )
        slope = dot(rows_ref[...], stacked, ((1,), (0,)))
        held.append(masked_rows(slope, lens_ref[...], weight_ref[...]))
    send_bands(table_ref, jnp.concatenate(held, axis=0), out_ref, buffer, sem)


def radial_slope(x, low, high, lens, weight, rows_map, table):
    rows = 2 * math.prod(x.shape[1:-1])
    return call(
        slope_kernel, "radial_slope", pltpu.HBM((R, rows), BF16), [HERE] * 7, FAR,
        [pltpu.VMEM((R, rows), BF16), pltpu.SemaphoreType.DMA((4,))],
    )(x, low, high, lens, weight, rows_map, table)


def sine_cosine(phase, points):
    centred = ((phase + points // 2) & (points - 1)) - points // 2
    y = centred.astype(F32) * (math.pi / points)
    square = y * y
    sine = jnp.float32(0.0)
    for n in (11, 9, 7, 5, 3, 1):
        sine = sine * square + (-1.0) ** (n // 2) / math.factorial(n)
    sine = sine * y
    cosine = jnp.float32(0.0)
    for n in (12, 10, 8, 6, 4, 2, 0):
        cosine = cosine * square + (-1.0) ** (n // 2) / math.factorial(n)
    return 1.0 - 2.0 * sine * sine, 2.0 * sine * cosine


def table_kernel(slots, orders_ref, out_ref):
    points = out_ref.shape[1]
    lane = lax.broadcasted_iota(jnp.int32, (slots, 128), 1)
    per_row = 128 // slots
    for row in range(orders_ref.shape[0]):
        column = jnp.broadcast_to(orders_ref[row:row + 1, :], (128, 128)).T
        for piece in range(per_row):
            orders = column[piece * slots:(piece + 1) * slots]
            start = (row * per_row + piece) * 2 * slots
            cos_now, sin_now = sine_cosine((orders * lane) & (points - 1), points)
            cos_turn, sin_turn = sine_cosine((orders * 128) & (points - 1), points)
            for block in range(points // 128):
                part = pl.ds(block * 128, 128)
                out_ref[start:start + slots, part] = cos_now.astype(BF16)
                out_ref[start + slots:start + 2 * slots, part] = (-sin_now).astype(BF16)
                cos_now, sin_now = (
                    cos_now * cos_turn - sin_now * sin_turn,
                    sin_now * cos_turn + cos_now * sin_turn,
                )


def azimuthal_table(orders, slots, points):
    return call(
        functools.partial(table_kernel, slots), "azimuthal_table",
        pltpu.VMEM((2 * orders.size, points), BF16), [HERE], HERE,
    )(orders)


def place_field(lhs, mapped, row, groups, band):
    width = mapped.shape[1] // 2
    low_lanes = lax.broadcasted_iota(jnp.int32, (band, width), 1) < width // 2
    for pair in range(groups // 2):
        even = mapped[2 * pair * band:(2 * pair + 1) * band]
        odd = mapped[(2 * pair + 1) * band:(2 * pair + 2) * band]
        first = jnp.where(low_lanes, even[:, :width], odd[:, width:])
        second = jnp.where(low_lanes, even[:, width:], odd[:, :width])
        cols = pl.ds(pair * width, width)
        lhs[row:row + band, cols] = first.astype(BF16)
        lhs[row + band:row + 2 * band, cols] = second.astype(BF16)


def axial_kernel(groups, band, step, raw_ref, low_ref, high_ref, both_ref, dz_ref, table_ref,
                 axial_ref, product_ref, lhs):
    width = both_ref.shape[0]
    joined = jnp.concatenate([raw_ref[:, 0:width], low_ref[...], high_ref[...]], axis=1)
    place_field(lhs, dot(joined, dz_ref[...], ((1,), (0,))), 0, groups, band)
    mapped = dot(raw_ref[:, width:2 * width], both_ref[...], ((1,), (0,)))
    place_field(lhs, mapped, 2 * band, groups, band)
    for start in range(0, table_ref.shape[1], step):
        part = pl.ds(start, step)
        values = dot(lhs[...], table_ref[:, part], ((1,), (0,)))
        axial = values[2 * band:] * (1.0 / 12.0)
        axial_ref[:, part] = axial
        product_ref[:, part] = (values[:2 * band] * axial).astype(BF16)


def axial_stage(raw, low, high, both, dz, table, groups, band, step=512):
    rows, points = table.shape
    return call(
        functools.partial(axial_kernel, groups, band, step), "axial_stage",
        (jax.ShapeDtypeStruct((2 * band, points), F32),
         jax.ShapeDtypeStruct((2 * band, points), BF16)),
        [HERE] * 6, (HERE, HERE), [pltpu.VMEM((4 * band, rows), BF16)],
    )(raw, low, high, both, dz, table)


def physical_kernel(groups, band, step, scale, slope_ref, axial_ref, product_ref, both_ref,
                    far_ref, out_ref, lhs, products, table_ref, sem):
    width = both_ref.shape[0]
    half = width // 2
    rows, points = table_ref.shape
    loads = []
    for block in range(points // step):
        for piece in range(4):
            area = (pl.ds(piece * (rows // 4), rows // 4), pl.ds(block * step, step))
            loads.append(pltpu.make_async_copy(
                far_ref.at[area], table_ref.at[area], sem.at[4 * block + piece]))
            loads[-1].start()
    for field in range(2):
        mapped = dot(slope_ref[:, field * width:(field + 1) * width], both_ref[...], ((1,), (0,)))
        place_field(lhs, mapped, 2 * field * band, groups, band)
    products[4 * band:6 * band, :] = product_ref[...]
    for start in range(0, points, step):
        part = pl.ds(start, step)
        for piece in range(4):
            loads[4 * (start // step) + piece].wait()
        values = dot(lhs[...], table_ref[:, part], ((1,), (0,)))
        axial = axial_ref[:, part]
        products[0:2 * band, part] = (values[:2 * band] * axial).astype(BF16)
        products[2 * band:4 * band, part] = (values[2 * band:] * axial).astype(BF16)

    low_lanes = lax.broadcasted_iota(jnp.int32, (band, width), 1) < half
    for start in range(0, rows, step):
        part = pl.ds(start, step)
        spectral = dot(products[...], table_ref[part, :], ((1,), (1,))) * scale
        for g in range(3):
            out_cols = pl.ds(g * width, width)
            for tile in range(step // width):
                cols = slice(tile * width, (tile + 1) * width)
                first = spectral[(2 * g) * band:(2 * g + 1) * band, cols]
                second = spectral[(2 * g + 1) * band:(2 * g + 2) * band, cols]
                even = jnp.where(low_lanes, first, pltpu.roll(second, half, 1))
                odd = jnp.where(low_lanes, pltpu.roll(first, half, 1), second)
                row = (start // width + tile) * 2 * band
                out_ref[row:row + band, out_cols] = even.astype(BF16)
                out_ref[row + band:row + 2 * band, out_cols] = odd.astype(BF16)


def physical_stage(slope, axial, product, both, table, groups, band, step=512):
    rows, points = table.shape
    width = both.shape[0]
    return call(
        functools.partial(physical_kernel, groups, band, step, math.sqrt(2.0 / points)),
        "physical_stage",
        jax.ShapeDtypeStruct((groups * band, 3 * width), BF16), [HERE] * 4 + [FAR], HERE,
        [pltpu.VMEM((4 * band, rows), BF16), pltpu.VMEM((6 * band, points), BF16),
         pltpu.VMEM(table.shape, BF16), pltpu.SemaphoreType.DMA((4 * (points // step),))],
        limit=28,
    )(slope, axial, product, both, in_hbm(table))


def final_kernel(x_ref, lens_ref, back_ref, table_ref, out_ref, buffer, sem):
    width = back_ref.shape[0]
    modes = lax.broadcasted_iota(jnp.int32, (width, table_ref.shape[1]), 1)
    keep = modes < lens_ref[:, :1]
    copies = []
    for g in range(3):
        mapped = dot(x_ref[:, g * width:(g + 1) * width], back_ref[...], ((1,), (0,)))
        result = dot(mapped.astype(BF16), table_ref[...], ((0,), (0,)))
        rows = jnp.where(keep, result, 0.0).astype(BF16)
        buffer[g] = rows.reshape(buffer.shape[1:])
        copies.append(pltpu.make_async_copy(buffer.at[g], out_ref.at[g], sem.at[g]))
        copies[-1].start()
    for copy in copies:
        copy.wait()


def radial_analysis(x, lens, back, table, shape):
    return call(
        final_kernel, "radial_analysis", pltpu.HBM(shape, BF16), [HERE] * 4, FAR,
        [pltpu.VMEM(shape, BF16), pltpu.SemaphoreType.DMA((3,))],
    )(x, lens, back, table)


def shift(block, offset):
    count = lax.axis_size("axial")
    return lax.ppermute(block, "axial", [(i, (i + offset) % count) for i in range(count)])


def exchange(block):
    return lax.all_to_all(block, "order", split_axis=0, concat_axis=0, tiled=True)


def shards(coefficients, order_lists, lengths):
    field_count, part_count, slots, planes, modes = coefficients.shape
    order_count = order_lists.shape[0]
    points = 2 * order_count
    groups = lax.axis_size("order")
    band = R // groups
    width = part_count * slots * planes
    synthesis, analysis = radial_constants(R, modes)
    rows_map, both, dz, back = plane_matrices(slots)

    sloped, raw = stage(coefficients)
    low, high = shift(sloped, 1), shift(sloped, -1)
    bands, lens, weight = radial_raw(order_lists, lengths, raw, synthesis)
    raw_bands = exchange(bands)
    table = azimuthal_table(order_lists.reshape(order_count // 128, 128), slots, points)
    own_band = raw_bands[:, :width]
    low_band, high_band = shift(own_band, 1), shift(own_band, -1)
    later_lens, table = lax.optimization_barrier((lens, table))
    slope_bands = exchange(
        radial_slope(sloped, low, high, later_lens, weight, rows_map, synthesis)
    )
    axial, product = axial_stage(raw_bands, low_band, high_band, both, dz, table, groups, band)
    spectral = physical_stage(slope_bands, axial, product, both, table, groups, band)
    shape = (3, part_count, slots, planes, modes)
    return radial_analysis(exchange(spectral), lens, back, analysis, shape)


def solution(mesh):
    placed = (P(None, None, "order", "axial", None), P(), P())
    return jax.shard_map(
        shards,
        mesh=mesh,
        in_specs=placed,
        out_specs=P(None, None, "order", "axial", None),
        check_vma=False,
    )
```

profile of v0, /device:TPU:1, one launch (start us, length us, event | category | flops | bytes accessed | tf_op | source)
XLA Modules:
  0.0 85.1 jit_solution(16963510228638827131)
XLA Ops:
  0.0 1.4 %stage.1 = (bf16[2,2,32,2,1024]{4,3,2,1,0:T(2,128)(2,1)S(1)}, bf16[2,2,32,2,1024]{4,3,2,1,0:T(2,128)(2,1)S(1)}) custom-call(bf16[4,2,32,2,1024]{4,3,2,1,0:T(2,128)(2,1)} %x_ref.1), custom_call_target="tpu_custom_call" | custom-call | tf_op jit(solution)/shard_map/stage/pallas_call | solution.py:90
  1.4 2.5 %collective-permute-start = (bf16[2,2,32,2,1024]{4,3,2,1,0:T(2,128)(2,1)S(1)}, bf16[2,2,32,2,1024]{4,3,2,1,0:T(2,128)(2,1)S(1)}, u32[]{:S(2)}, u32[]{:S(2)}) collective-permute-start(bf16[2,2,32,2,1024]{4,3,2,1,0:T(2,128)(2,1)S(1)} %get-tuple-element.14.x_ref), channel_id=1, source_target_pairs={{0,1},{1,2},{2,3},{3,4},{4,5},{5,6},{6,7},{7,0},{8,9},{9,10},{10,1... | collective-permute-start | bytes 1572872 | tf_op jit(solution)/shard_map/ppermute | solution.py:343
  3.9 4.0 %collective-permute-start.1 = (bf16[2,2,32,2,1024]{4,3,2,1,0:T(2,128)(2,1)S(1)}, bf16[2,2,32,2,1024]{4,3,2,1,0:T(2,128)(2,1)S(1)}, u32[]{:S(2)}, u32[]{:S(2)}) collective-permute-start(bf16[2,2,32,2,1024]{4,3,2,1,0:T(2,128)(2,1)S(1)} %get-tuple-element.14.x_ref), channel_id=1, source_target_pairs={{0,7},{1,0},{2,1},{3,2},{4,3},{5,4},{6,5},{7,6},{8,15},{9,8},{10,9... | collective-permute-start | bytes 1572872 | tf_op jit(solution)/shard_map/ppermute | solution.py:343
  7.9 0.7 copy-done.8
  8.6 0.7 copy-done.10
  9.3 4.3 %radial_raw.1 = (bf16[1024,256]{1,0:T(8,128)(2,1)}, s32[128,128]{1,0:T(8,128)S(1)}, f32[128,128]{1,0:T(8,128)S(1)}) custom-call(s32[1024]{0:T(1024)S(1)} %copy-done.8, s32[1024]{0:T(1024)S(1)} %copy-done.10, bf16[2,2,32,2,1024]{4,3,2,1,0:T(2,128)(2,1)S(1)} %get-tuple-element.15.x_ref, bf16[1024,1024]{1,0:T(8,128)(2,1)} %constant.12.clone.table_ref), custom_call_target="tpu_custom_call" | custom-call | tf_op jit(solution)/shard_map/radial_raw/pallas_call | solution.py:151
  13.6 8.1 %all-to-all-start.1 = ((bf16[32,32,256]{2,1,0:T(8,128)(2,1)}), bf16[32,32,256]{2,1,0:T(8,128)(2,1)S(1)}, u32[]{:S(2)}, u32[]{:S(2)}) async-start(bf16[32,32,256]{2,1,0:T(8,128)(2,1)} %bitcast.14), calls=%async_computation.1 | async-start | bytes 1048576 | tf_op jit(solution)/shard_map/all_to_all | solution.py:347
  21.7 0.0 copy-done.9
  21.7 0.0 copy-start.2
  21.7 0.0 copy-start.6
  21.7 4.0 %azimuthal_table.1.table_ref.far_ref = bf16[2048,2048]{1,0:T(8,128)(2,1)S(1)} custom-call(s32[8,128]{1,0:T(8,128)S(1)} %bitcast.12), custom_call_target="tpu_custom_call" | custom-call | tf_op jit(solution)/shard_map/azimuthal_table/pallas_call | solution.py:219
  25.7 0.0 copy-start
  25.7 3.2 %copy-done = bf16[2048,2048]{1,0:T(8,128)(2,1)} copy-done((bf16[2048,2048]{1,0:T(8,128)(2,1)}, bf16[2048,2048]{1,0:T(8,128)(2,1)S(1)}, u32[]{:S(2)}) %copy-start) | copy-done | bytes 8388632
  28.9 0.0 collective-permute-done.low_ref
  28.9 0.0 collective-permute-done.1.high_ref
  29.0 0.0 copy-start.4
  29.0 0.0 copy-start.5
  29.0 1.9 %radial_slope.1 = bf16[1024,256]{1,0:T(8,128)(2,1)} custom-call(bf16[2,2,32,2,1024]{4,3,2,1,0:T(2,128)(2,1)S(1)} %get-tuple-element.14.x_ref, bf16[2,2,32,2,1024]{4,3,2,1,0:T(2,128)(2,1)S(1)} %collective-permute-done.low_ref, bf16[2,2,32,2,1024]{4,3,2,1,0:T(2,128)(2,1)S(1)} %collective-permute-done.1.high_ref, s32[128,128]{1,0:T(8,128)S(1)} %get-tuple-element.17.lens_ref, ...), custom_call_target="tpu_custom_call" | custom-call | tf_op jit(solution)/shard_map/radial_slope/pallas_call | solution.py:177
  30.9 2.4 %all-to-all-done.1 = bf16[32,32,256]{2,1,0:T(8,128)(2,1)S(1)} async-done(((bf16[32,32,256]{2,1,0:T(8,128)(2,1)}), bf16[32,32,256]{2,1,0:T(8,128)(2,1)S(1)}, u32[]{:S(2)}, u32[]{:S(2)}) %all-to-all-start.1) | async-done | bytes 524320 | tf_op jit(solution)/shard_map/all_to_all | solution.py:347
  33.3 4.9 %all-to-all-start = ((bf16[32,32,256]{2,1,0:T(8,128)(2,1)}), bf16[32,32,256]{2,1,0:T(8,128)(2,1)S(1)}, u32[]{:S(2)}, u32[]{:S(2)}) async-start(bf16[32,32,256]{2,1,0:T(8,128)(2,1)} %bitcast.13), calls=%async_computation | async-start | bytes 1048576 | tf_op jit(solution)/shard_map/all_to_all | solution.py:347
  38.3 0.1 collective-permute-start.2
  38.4 2.7 %collective-permute-start.3 = (bf16[1024,128]{1,0:T(8,128)(2,1)S(1)}, bf16[1024,128]{1,0:T(8,128)(2,1)S(1)}, u32[]{:S(2)}, u32[]{:S(2)}) collective-permute-start(bf16[1024,128]{1,0:T(8,128)(2,1)S(1)} %slice.4), channel_id=1, source_target_pairs={{0,7},{1,0},{2,1},{3,2},{4,3},{5,4},{6,5},{7,6},{8,15},{9,8},{10,9... | collective-permute-start | bytes 786440 | tf_op jit(solution)/shard_map/ppermute | solution.py:343
  41.0 6.2 %collective-permute-done.2.low_ref = bf16[1024,128]{1,0:T(8,128)(2,1)S(1)} collective-permute-done((bf16[1024,128]{1,0:T(8,128)(2,1)S(1)}, bf16[1024,128]{1,0:T(8,128)(2,1)S(1)}, u32[]{:S(2)}, u32[]{:S(2)}) %collective-permute-start.2) | collective-permute-done | bytes 262176 | tf_op jit(solution)/shard_map/ppermute | solution.py:343
  47.2 0.0 collective-permute-done.3.high_ref
  47.3 3.4 %copy-done.1 = bf16[2048,2048]{1,0:T(8,128)(2,1)S(1)} copy-done((bf16[2048,2048]{1,0:T(8,128)(2,1)S(1)}, bf16[2048,2048]{1,0:T(8,128)(2,1)}, u32[]{:S(2)}) %copy-start.1) | copy-done | bytes 8388632
  50.6 2.2 %axial_stage.1 = (f32[64,2048]{1,0:T(8,128)S(1)}, bf16[64,2048]{1,0:T(8,128)(2,1)S(1)}) custom-call(bf16[1024,256]{1,0:T(8,128)(2,1)S(1)} %bitcast.8, bf16[1024,128]{1,0:T(8,128)(2,1)S(1)} %collective-permute-done.2.low_ref, bf16[1024,128]{1,0:T(8,128)(2,1)S(1)} %collective-permute-done.3.high_ref, bf16[128,256]{1,0:T(8,128)(2,1)S(1)} %copy-done.4, ...), custom_call_target="tpu_custom_call" | custom-call | tf_op jit(solution)/shard_map/axial_stage/pallas_call | solution.py:255
  52.9 0.0 all-to-all-done
  52.9 0.0 copy-start.3
  52.9 0.0 copy-start.7
  52.9 7.3 %physical_stage.1 = bf16[1024,384]{1,0:T(8,128)(2,1)S(1)} custom-call(bf16[1024,256]{1,0:T(8,128)(2,1)S(1)} %bitcast.11, f32[64,2048]{1,0:T(8,128)S(1)} %get-tuple-element.21.axial_ref, bf16[64,2048]{1,0:T(8,128)(2,1)S(1)} %get-tuple-element.22.product_ref, bf16[128,256]{1,0:T(8,128)(2,1)S(1)} %copy-done.4, bf16[2048,2048]{1,0:T(8,128)(2,1)} %copy-done), custom_call_target="tpu_custom_call" | custom-call | tf_op jit(solution)/shard_map/physical_stage/pallas_call | solution.py:308
  60.2 22.1 %all_to_all.33 = bf16[32,32,384]{2,1,0:T(8,128)(2,1)S(1)} all-to-all(bf16[32,32,384]{2,1,0:T(8,128)(2,1)S(1)} %bitcast.9), channel_id=1, replica_groups=mesh['order'=32,'axial'=8] {'order'}, dimensions={0} | all-to-all | bytes 1572864 | tf_op jit(solution)/shard_map/all_to_all | solution.py:347
  82.3 2.6 %radial_analysis.1 = bf16[3,2,32,2,1024]{4,3,2,1,0:T(2,128)(2,1)} custom-call(bf16[1024,384]{1,0:T(8,128)(2,1)S(1)} %bitcast.10, s32[128,128]{1,0:T(8,128)S(1)} %get-tuple-element.17.lens_ref, bf16[128,128]{1,0:T(8,128)(2,1)S(1)} %copy-done.7, bf16[1024,1024]{1,0:T(8,128)(2,1)S(1)} %copy-done.3), custom_call_target="tpu_custom_call" | custom-call | tf_op jit(solution)/shard_map/radial_analysis/pallas_call | solution.py:335
  (11 shorter events, 0.0 us)
Async XLA Ops:
  0.0 21.7 %copy-start.9 = (s32[1024]{0:T(1024)S(1)}, s32[1024]{0:T(1024)}, u32[]{:S(2)}) copy-start(s32[1024]{0:T(1024)} %orders_ref.1) | copy-start | bytes 12292
  1.4 27.6 %collective-permute-start = (bf16[2,2,32,2,1024]{4,3,2,1,0:T(2,128)(2,1)S(1)}, bf16[2,2,32,2,1024]{4,3,2,1,0:T(2,128)(2,1)S(1)}, u32[]{:S(2)}, u32[]{:S(2)}) collective-permute-start(bf16[2,2,32,2,1024]{4,3,2,1,0:T(2,128)(2,1)S(1)} %get-tuple-element.14.x_ref), channel_id=1, source_target_pairs={{0,1},{1,2},{2,3},{3,4},{4,5},{5,6},{6,7},{7,0},{8,9},{9,10},{10,1... | collective-permute-start | bytes 1572872 | tf_op jit(solution)/shard_map/ppermute | solution.py:343
  3.9 25.0 %collective-permute-start.1 = (bf16[2,2,32,2,1024]{4,3,2,1,0:T(2,128)(2,1)S(1)}, bf16[2,2,32,2,1024]{4,3,2,1,0:T(2,128)(2,1)S(1)}, u32[]{:S(2)}, u32[]{:S(2)}) collective-permute-start(bf16[2,2,32,2,1024]{4,3,2,1,0:T(2,128)(2,1)S(1)} %get-tuple-element.14.x_ref), channel_id=1, source_target_pairs={{0,7},{1,0},{2,1},{3,2},{4,3},{5,4},{6,5},{7,6},{8,15},{9,8},{10,9... | collective-permute-start | bytes 1572872 | tf_op jit(solution)/shard_map/ppermute | solution.py:343
  7.9 0.7 copy-start.8
  8.6 0.7 copy-start.10
  13.6 19.7 %all-to-all-start.1 = ((bf16[32,32,256]{2,1,0:T(8,128)(2,1)}), bf16[32,32,256]{2,1,0:T(8,128)(2,1)S(1)}, u32[]{:S(2)}, u32[]{:S(2)}) async-start(bf16[32,32,256]{2,1,0:T(8,128)(2,1)} %bitcast.14), calls=%async_computation.1 | async-start | bytes 1048576 | tf_op jit(solution)/shard_map/all_to_all | solution.py:347
  21.7 7.2 %copy-start.2 = (bf16[1024,1024]{1,0:T(8,128)(2,1)S(1)}, bf16[1024,1024]{1,0:T(8,128)(2,1)}, u32[]{:S(2)}) copy-start(bf16[1024,1024]{1,0:T(8,128)(2,1)} %constant.12.clone.table_ref) | copy-start | bytes 6291460
  21.7 7.2 %copy-start.6 = (bf16[128,384]{1,0:T(8,128)(2,1)S(1)}, bf16[128,384]{1,0:T(8,128)(2,1)}, u32[]{:S(2)}) copy-start(bf16[128,384]{1,0:T(8,128)(2,1)} %constant.13.clone.rows_ref) | copy-start | bytes 294916
  25.7 3.2 %copy-start = (bf16[2048,2048]{1,0:T(8,128)(2,1)}, bf16[2048,2048]{1,0:T(8,128)(2,1)S(1)}, u32[]{:S(2)}) copy-start(bf16[2048,2048]{1,0:T(8,128)(2,1)S(1)} %azimuthal_table.1.table_ref.far_ref) | copy-start | bytes 25165828
  29.0 18.3 %copy-start.4 = (bf16[128,256]{1,0:T(8,128)(2,1)S(1)}, bf16[128,256]{1,0:T(8,128)(2,1)}, u32[]{:S(2)}) copy-start(bf16[128,256]{1,0:T(8,128)(2,1)} %constant.14.clone.both_ref) | copy-start | bytes 196612
  29.0 18.3 %copy-start.5 = (bf16[384,256]{1,0:T(8,128)(2,1)S(1)}, bf16[384,256]{1,0:T(8,128)(2,1)}, u32[]{:S(2)}) copy-start(bf16[384,256]{1,0:T(8,128)(2,1)} %constant.15.clone.dz_ref) | copy-start | bytes 589828
  33.3 19.6 %all-to-all-start = ((bf16[32,32,256]{2,1,0:T(8,128)(2,1)}), bf16[32,32,256]{2,1,0:T(8,128)(2,1)S(1)}, u32[]{:S(2)}, u32[]{:S(2)}) async-start(bf16[32,32,256]{2,1,0:T(8,128)(2,1)} %bitcast.13), calls=%async_computation | async-start | bytes 1048576 | tf_op jit(solution)/shard_map/all_to_all | solution.py:347
  38.3 9.0 %collective-permute-start.2 = (bf16[1024,128]{1,0:T(8,128)(2,1)S(1)}, bf16[1024,128]{1,0:T(8,128)(2,1)S(1)}, u32[]{:S(2)}, u32[]{:S(2)}) collective-permute-start(bf16[1024,128]{1,0:T(8,128)(2,1)S(1)} %slice.4), channel_id=1, source_target_pairs={{0,1},{1,2},{2,3},{3,4},{4,5},{5,6},{6,7},{7,0},{8,9},{9,10},{10,1... | collective-permute-start | bytes 786440 | tf_op jit(solution)/shard_map/ppermute | solution.py:343
  38.4 8.9 %collective-permute-start.3 = (bf16[1024,128]{1,0:T(8,128)(2,1)S(1)}, bf16[1024,128]{1,0:T(8,128)(2,1)S(1)}, u32[]{:S(2)}, u32[]{:S(2)}) collective-permute-start(bf16[1024,128]{1,0:T(8,128)(2,1)S(1)} %slice.4), channel_id=1, source_target_pairs={{0,7},{1,0},{2,1},{3,2},{4,3},{5,4},{6,5},{7,6},{8,15},{9,8},{10,9... | collective-permute-start | bytes 786440 | tf_op jit(solution)/shard_map/ppermute | solution.py:343
  47.3 3.4 %copy-start.1 = (bf16[2048,2048]{1,0:T(8,128)(2,1)S(1)}, bf16[2048,2048]{1,0:T(8,128)(2,1)}, u32[]{:S(2)}) copy-start(bf16[2048,2048]{1,0:T(8,128)(2,1)} %copy-done) | copy-start | bytes 25165828
  52.9 29.4 %copy-start.3 = (bf16[1024,1024]{1,0:T(8,128)(2,1)S(1)}, bf16[1024,1024]{1,0:T(8,128)(2,1)}, u32[]{:S(2)}) copy-start(bf16[1024,1024]{1,0:T(8,128)(2,1)} %constant.17.clone.table_ref) | copy-start | bytes 6291460
  52.9 29.4 %copy-start.7 = (bf16[128,128]{1,0:T(8,128)(2,1)S(1)}, bf16[128,128]{1,0:T(8,128)(2,1)}, u32[]{:S(2)}) copy-start(bf16[128,128]{1,0:T(8,128)(2,1)} %constant.16.clone.back_ref) | copy-start | bytes 98308
where the time goes:
time: 85.5 us; the launch traced here: 85.1 us
  Pallas kernels  23.6 us (28%)
  starting transfers between devices  22.3 us (26%)
  blocking collectives  22.1 us (26%)
  waiting for transfers between devices  8.67 us (10%)
  local copies, waits for them, and re-layouts  8.05 us (9%)
    all_to_all x1, blocking collectives, exchange(): lax.all_to_all(block, 'order', split_axis=0, concat_axis=0, tiled=True)  22.1 us
    all_to_all x2, starting transfers between devices, exchange(): lax.all_to_all(block, 'order', split_axis=0, concat_axis=0, tiled=True)  13 us
    ppermute x4, starting transfers between devices, shift(): lax.ppermute(block, 'axial', [(i, (i + offset) % count) for i in range(co...  9.32 us
    unnamed x22, local copies, waits for them, and re-layouts  8.03 us
    pallas_call x1, Pallas kernels, physical_stage(): call(functools.partial(physical_kernel, groups, band, step, math.sqrt(2.0...  7.31 us
    ppermute x4, waiting for transfers between devices, shift(): lax.ppermute(block, 'axial', [(i, (i + offset) % count) for i in range(co...  6.21 us
    pallas_call x1, Pallas kernels, radial_raw(): call(functools.partial(raw_kernel, x.shape[2]), 'radial_raw', (pltpu.HBM(...  4.3 us
    pallas_call x1, Pallas kernels, azimuthal_table(): call(functools.partial(table_kernel, slots), 'azimuthal_table', pltpu.VME...  3.96 us
  transfers between devices with their start and end apart: 6, of which 2 were waited for; matrix products, arithmetic and copies ran while one was open for 0% of the time, Pallas kernels for 15%

commit v1 on v0

--- a/solution.py
+++ b/solution.py
@@ -38,11 +38,9 @@
     rows = np.concatenate([own, low, high], axis=1)
     swap = np.roll(np.eye(width, dtype=np.float32), pair, axis=1)
     both = np.concatenate([gather, gather @ swap], axis=1)
-    slope = rows.T @ both
     return (
         rows.astype(jnp.bfloat16),
         both.astype(jnp.bfloat16),
-        slope.astype(jnp.bfloat16),
         gather.T.astype(jnp.bfloat16),
     )
 
@@ -72,25 +70,24 @@
     )
 
 
-def stage_kernel(x_ref, slope_ref, raw_ref, sem):
+def stage_kernel(x_ref, out_ref, sem):
+    fields, parts, slots = out_ref.shape[:3]
     copies = []
-    for field in range(4):
-        target = slope_ref if field < 2 else raw_ref
-        for part in range(2):
-            copies.append(pltpu.make_async_copy(
-                x_ref.at[field, part], target.at[field % 2, part], sem.at[2 * field + part]))
-    for copy in copies:
-        copy.start()
+    for field in range(fields):
+        for part in range(parts):
+            for half in range(2):
+                area = (field, part, pl.ds(half * (slots // 2), slots // 2))
+                copies.append(pltpu.make_async_copy(
+                    x_ref.at[area], out_ref.at[area], sem.at[len(copies)]))
+                copies[-1].start()
     for copy in copies:
         copy.wait()
 
 
 def stage(x):
-    half = (2,) + x.shape[1:]
-    return call(
-        stage_kernel, "stage",
-        (pltpu.VMEM(half, BF16), pltpu.VMEM(half, BF16)),
-        [FAR], (HERE, HERE), [pltpu.SemaphoreType.DMA((8,))],
+    return call(
+        stage_kernel, "stage", pltpu.VMEM((3,) + x.shape[1:], BF16),
+        [FAR], HERE, [pltpu.SemaphoreType.DMA((12,))],
     )(in_hbm(x))
 
 
@@ -118,51 +115,75 @@
         copy.wait()
 
 
-def raw_kernel(slots, orders_ref, lengths_ref, x_ref, table_ref, out_ref, lens_ref, weight_ref,
-               buffer, sem, held_table, load_sem):
-    size = held_table.shape[0] // 4
+def slot_rows(orders, lengths, slots):
+    index = lax.axis_index("order")
+    per_row = 128 // slots
+    lane = lax.broadcasted_iota(jnp.int32, (128, 128), 1)
+    held = jnp.broadcast_to(orders[pl.ds(index // per_row, 1), :], (128, 128)).T
+    total = jnp.zeros((128, 128), F32)
+    for row in range(lengths.shape[0]):
+        wide = jnp.broadcast_to(lengths[row:row + 1, :], (128, 128)).astype(F32)
+        total += jnp.where(held == lane + row * 128, wide, 0.0)
+    found = jnp.sum(total, axis=1, keepdims=True).astype(jnp.int32)
+    found = jnp.broadcast_to(found, (128, 128))
+    zero = jnp.where(held == 0, 1, 0)
+    columns = jnp.where(lane == 0, found >> 3, jnp.where(lane == 1, found & 7, zero))
+    rows = lax.broadcasted_iota(jnp.int32, (2 * slots, 128), 0) // 2
+    picked = lax.broadcasted_iota(jnp.int32, (2 * slots, 128), 1)
+    pick = jnp.where(picked == rows + (index % per_row) * slots, 1.0, 0.0).astype(BF16)
+    result = dot(pick, columns.astype(F32).astype(BF16), ((1,), (0,)))
+    lens = (result[:, 0:1] * 8.0 + result[:, 1:2]).astype(jnp.int32)
+    weight = 2.0 - result[:, 2:3]
+    return jnp.concatenate([lens, lens], axis=0), jnp.concatenate([weight, weight], axis=0)
+
+
+def raw_kernel(orders_far, lengths_far, x_far, table_far, out_ref, lens_ref, weight_ref,
+               buffer, sem, orders, lengths, x_ref, small_sem, table, load_sem):
+    size = table.shape[0] // 4
+    small = [
+        pltpu.make_async_copy(orders_far, orders, small_sem.at[0]),
+        pltpu.make_async_copy(lengths_far, lengths, small_sem.at[1]),
+        pltpu.make_async_copy(x_far.at[3, 0], x_ref.at[0], small_sem.at[2]),
+        pltpu.make_async_copy(x_far.at[3, 1], x_ref.at[1], small_sem.at[3]),
+    ]
     loads = [
-        pltpu.make_async_copy(table_ref.at[pl.ds(i * size, size)],
-                              held_table.at[pl.ds(i * size, size)], load_sem.at[i])
+        pltpu.make_async_copy(table_far.at[pl.ds(i * size, size)],
+                              table.at[pl.ds(i * size, size)], load_sem.at[i])
         for i in range(4)
     ]
-    for load in loads:
-        load.start()
-    base = lax.axis_index("order") * slots
-    rows = 2 * slots
-    slot_of = lax.broadcasted_iota(jnp.int32, (rows, 128), 0) // 2
-    lens = jnp.zeros((rows, 128), jnp.int32)
-    order = jnp.zeros((rows, 128), jnp.int32)
-    for slot in range(slots):
-        here = orders_ref[base + slot]
-        lens = jnp.where(slot_of == slot, lengths_ref[here], lens)
-        order = jnp.where(slot_of == slot, here, order)
-    lens = jnp.concatenate([lens, lens], axis=0)
-    weight = jnp.where(order == 0, 1.0, 2.0).astype(F32)
-    weight = jnp.concatenate([weight, weight], axis=0)
-    lens_ref[...] = lens
-    weight_ref[...] = weight
-    held = [masked_rows(field_rows(x_ref, field), lens, weight) for field in range(2)]
-    send_bands(held_table, jnp.concatenate(held, axis=0), out_ref, buffer, sem, loads)
+    for copy in small + loads:
+        copy.start()
+    small[0].wait()
+    small[1].wait()
+    lens, weight = slot_rows(orders, lengths, x_ref.shape[1])
+    lens_ref[...] = jnp.broadcast_to(lens, lens_ref.shape)
+    weight_ref[...] = jnp.broadcast_to(weight, weight_ref.shape)
+    small[2].wait()
+    small[3].wait()
+    block = x_ref[...]
+    block = block.reshape(math.prod(block.shape[:-1]), block.shape[-1])
+    send_bands(table, masked_rows(block, lens, weight), out_ref, buffer, sem, loads)
 
 
 def radial_raw(orders, lengths, x, table):
-    rows = 2 * math.prod(x.shape[1:-1])
-    return call(
-        functools.partial(raw_kernel, x.shape[2]), "radial_raw",
+    rows = math.prod(x.shape[1:-1])
+    return call(
+        raw_kernel, "radial_raw",
         (pltpu.HBM((R, rows), BF16),
-         jax.ShapeDtypeStruct((rows // 2, 128), jnp.int32),
-         jax.ShapeDtypeStruct((rows // 2, 128), F32)),
-        [SCALARS, SCALARS, HERE, FAR], (FAR, HERE, HERE),
+         jax.ShapeDtypeStruct((rows, 128), jnp.int32),
+         jax.ShapeDtypeStruct((rows, 128), F32)),
+        [FAR] * 4, (FAR, HERE, HERE),
         [pltpu.VMEM((R, rows), BF16), pltpu.SemaphoreType.DMA((4,)),
+         pltpu.VMEM(orders.shape, jnp.int32), pltpu.VMEM(lengths.shape, jnp.int32),
+         pltpu.VMEM(x.shape[1:], BF16), pltpu.SemaphoreType.DMA((4,)),
          pltpu.VMEM(table.shape, BF16), pltpu.SemaphoreType.DMA((4,))],
-    )(orders, lengths, x, in_hbm(table))
+    )(in_hbm(orders), in_hbm(lengths), in_hbm(x), in_hbm(table))
 
 
 def slope_kernel(x_ref, low_ref, high_ref, lens_ref, weight_ref, rows_ref, table_ref, out_ref,
                  buffer, sem):
     held = []
-    for field in range(2):
+    for field in range(3):
         stacked = jnp.concatenate(
             [field_rows(x_ref, field), field_rows(low_ref, field), field_rows(high_ref, field)],
             axis=0,
@@ -173,7 +194,7 @@
 
 
 def radial_slope(x, low, high, lens, weight, rows_map, table):
-    rows = 2 * math.prod(x.shape[1:-1])
+    rows = math.prod(x.shape[:-1])
     return call(
         slope_kernel, "radial_slope", pltpu.HBM((R, rows), BF16), [HERE] * 7, FAR,
         [pltpu.VMEM((R, rows), BF16), pltpu.SemaphoreType.DMA((4,))],
@@ -194,8 +215,9 @@
     return 1.0 - 2.0 * sine * sine, 2.0 * sine * cosine
 
 
-def table_kernel(slots, orders_ref, out_ref):
+def table_kernel(slots, orders_ref, far_ref, out_ref, sem):
     points = out_ref.shape[1]
+    copies = []
     lane = lax.broadcasted_iota(jnp.int32, (slots, 128), 1)
     per_row = 128 // slots
     for row in range(orders_ref.shape[0]):
@@ -213,12 +235,19 @@
                     cos_now * cos_turn - sin_now * sin_turn,
                     sin_now * cos_turn + cos_now * sin_turn,
                 )
+        part = pl.ds(row * 256, 256)
+        copies.append(pltpu.make_async_copy(out_ref.at[part], far_ref.at[part], sem.at[row]))
+        copies[-1].start()
+    for copy in copies:
+        copy.wait()
 
 
 def azimuthal_table(orders, slots, points):
     return call(
         functools.partial(table_kernel, slots), "azimuthal_table",
-        pltpu.VMEM((2 * orders.size, points), BF16), [HERE], HERE,
+        pltpu.HBM((2 * orders.size, points), BF16), [HERE], FAR,
+        [pltpu.VMEM((2 * orders.size, points), BF16),
+         pltpu.SemaphoreType.DMA((orders.shape[0],))],
     )(orders)
 
 
@@ -235,55 +264,59 @@
         lhs[row + band:row + 2 * band, cols] = second.astype(BF16)
 
 
-def axial_kernel(groups, band, step, raw_ref, low_ref, high_ref, both_ref, dz_ref, table_ref,
-                 axial_ref, product_ref, lhs):
-    width = both_ref.shape[0]
-    joined = jnp.concatenate([raw_ref[:, 0:width], low_ref[...], high_ref[...]], axis=1)
-    place_field(lhs, dot(joined, dz_ref[...], ((1,), (0,))), 0, groups, band)
-    mapped = dot(raw_ref[:, width:2 * width], both_ref[...], ((1,), (0,)))
-    place_field(lhs, mapped, 2 * band, groups, band)
-    for start in range(0, table_ref.shape[1], step):
-        part = pl.ds(start, step)
-        values = dot(lhs[...], table_ref[:, part], ((1,), (0,)))
-        axial = values[2 * band:] * (1.0 / 12.0)
-        axial_ref[:, part] = axial
-        product_ref[:, part] = (values[:2 * band] * axial).astype(BF16)
-
-
-def axial_stage(raw, low, high, both, dz, table, groups, band, step=512):
+def table_loads(far_ref, table_ref, sem, step):
+    rows, points = table_ref.shape
+    loads = []
+    for block in range(points // step):
+        loads.append([])
+        for piece in range(4):
+            area = (pl.ds(piece * (rows // 4), rows // 4), pl.ds(block * step, step))
+            loads[-1].append(pltpu.make_async_copy(
+                far_ref.at[area], table_ref.at[area], sem.at[4 * block + piece]))
+            loads[-1][-1].start()
+    return loads
+
+
+def axial_kernel(groups, band, step, raw_ref, both_ref, far_ref, axial_ref, lhs, table_ref, sem):
+    loads = table_loads(far_ref, table_ref, sem, step)
+    place_field(lhs, dot(raw_ref[...], both_ref[...], ((1,), (0,))), 0, groups, band)
+    for block in range(table_ref.shape[1] // step):
+        part = pl.ds(block * step, step)
+        for load in loads[block]:
+            load.wait()
+        axial_ref[:, part] = dot(lhs[...], table_ref[:, part], ((1,), (0,))) * (1.0 / 12.0)
+
+
+def axial_stage(raw, both, table, groups, band, step=512):
     rows, points = table.shape
     return call(
         functools.partial(axial_kernel, groups, band, step), "axial_stage",
-        (jax.ShapeDtypeStruct((2 * band, points), F32),
-         jax.ShapeDtypeStruct((2 * band, points), BF16)),
-        [HERE] * 6, (HERE, HERE), [pltpu.VMEM((4 * band, rows), BF16)],
-    )(raw, low, high, both, dz, table)
-
-
-def physical_kernel(groups, band, step, scale, slope_ref, axial_ref, product_ref, both_ref,
-                    far_ref, out_ref, lhs, products, table_ref, sem):
+        jax.ShapeDtypeStruct((2 * band, points), F32),
+        [HERE, HERE, FAR], HERE,
+        [pltpu.VMEM((2 * band, rows), BF16), pltpu.VMEM(table.shape, BF16),
+         pltpu.SemaphoreType.DMA((4 * (points // step),))],
+        limit=20,
+    )(raw, both, in_hbm(table))
+
+
+def physical_kernel(groups, band, step, scale, slope_ref, axial_ref, both_ref, far_ref, out_ref,
+                    lhs, products, table_ref, sem):
     width = both_ref.shape[0]
     half = width // 2
     rows, points = table_ref.shape
-    loads = []
-    for block in range(points // step):
-        for piece in range(4):
-            area = (pl.ds(piece * (rows // 4), rows // 4), pl.ds(block * step, step))
-            loads.append(pltpu.make_async_copy(
-                far_ref.at[area], table_ref.at[area], sem.at[4 * block + piece]))
-            loads[-1].start()
-    for field in range(2):
+    loads = table_loads(far_ref, table_ref, sem, step)
+    for field in range(3):
         mapped = dot(slope_ref[:, field * width:(field + 1) * width], both_ref[...], ((1,), (0,)))
         place_field(lhs, mapped, 2 * field * band, groups, band)
-    products[4 * band:6 * band, :] = product_ref[...]
-    for start in range(0, points, step):
-        part = pl.ds(start, step)
-        for piece in range(4):
-            loads[4 * (start // step) + piece].wait()
+    for block in range(points // step):
+        part = pl.ds(block * step, step)
+        for load in loads[block]:
+            load.wait()
         values = dot(lhs[...], table_ref[:, part], ((1,), (0,)))
         axial = axial_ref[:, part]
-        products[0:2 * band, part] = (values[:2 * band] * axial).astype(BF16)
-        products[2 * band:4 * band, part] = (values[2 * band:] * axial).astype(BF16)
+        for g in range(3):
+            area = slice(2 * g * band, (2 * g + 2) * band)
+            products[area, part] = (values[area] * axial).astype(BF16)
 
     low_lanes = lax.broadcasted_iota(jnp.int32, (band, width), 1) < half
     for start in range(0, rows, step):
@@ -302,17 +335,17 @@
                 out_ref[row + band:row + 2 * band, out_cols] = odd.astype(BF16)
 
 
-def physical_stage(slope, axial, product, both, table, groups, band, step=512):
+def physical_stage(slope, axial, both, table, groups, band, step=512):
     rows, points = table.shape
     width = both.shape[0]
     return call(
         functools.partial(physical_kernel, groups, band, step, math.sqrt(2.0 / points)),
         "physical_stage",
-        jax.ShapeDtypeStruct((groups * band, 3 * width), BF16), [HERE] * 4 + [FAR], HERE,
-        [pltpu.VMEM((4 * band, rows), BF16), pltpu.VMEM((6 * band, points), BF16),
+        jax.ShapeDtypeStruct((groups * band, 3 * width), BF16), [HERE] * 3 + [FAR], HERE,
+        [pltpu.VMEM((6 * band, rows), BF16), pltpu.VMEM((6 * band, points), BF16),
          pltpu.VMEM(table.shape, BF16), pltpu.SemaphoreType.DMA((4 * (points // step),))],
         limit=28,
-    )(slope, axial, product, both, in_hbm(table))
+    )(slope, axial, both, in_hbm(table))
 
 
 def final_kernel(x_ref, lens_ref, back_ref, table_ref, out_ref, buffer, sem):
@@ -355,21 +388,22 @@
     band = R // groups
     width = part_count * slots * planes
     synthesis, analysis = radial_constants(R, modes)
-    rows_map, both, dz, back = plane_matrices(slots)
-
-    sloped, raw = stage(coefficients)
+    rows_map, both, back = plane_matrices(slots)
+
+    sloped = stage(coefficients)
     low, high = shift(sloped, 1), shift(sloped, -1)
-    bands, lens, weight = radial_raw(order_lists, lengths, raw, synthesis)
+    orders = order_lists.reshape(order_count // 128, 128)
+    bands, lens, weight = radial_raw(
+        orders, lengths.reshape(order_count // 128, 128), coefficients, synthesis
+    )
     raw_bands = exchange(bands)
-    table = azimuthal_table(order_lists.reshape(order_count // 128, 128), slots, points)
-    own_band = raw_bands[:, :width]
-    low_band, high_band = shift(own_band, 1), shift(own_band, -1)
+    table = azimuthal_table(orders, slots, points)
     later_lens, table = lax.optimization_barrier((lens, table))
     slope_bands = exchange(
         radial_slope(sloped, low, high, later_lens, weight, rows_map, synthesis)
     )
-    axial, product = axial_stage(raw_bands, low_band, high_band, both, dz, table, groups, band)
-    spectral = physical_stage(slope_bands, axial, product, both, table, groups, band)
+    axial = axial_stage(raw_bands, both, table, groups, band)
+    spectral = physical_stage(slope_bands, axial, both, table, groups, band)
     shape = (3, part_count, slots, planes, modes)
     return radial_analysis(exchange(spectral), lens, back, analysis, shape)
 

time: 85.5 us -> 81.4 us (0.952)
  local copies, waits for them, and re-layouts: 8.05 us -> 0.03 us
  blocking collectives: 22.1 us -> 17.9 us
  Pallas kernels: 23.6 us -> 27.2 us
  waiting for transfers between devices: 8.67 us -> 12.1 us
  starting transfers between devices: 22.3 us -> 23.5 us
    unnamed x22 -> x12, local copies, waits for them, and re-layouts: 8.03 us -> 0.03 us
    all_to_all x2, waiting for transfers between devices: 2.45 us -> 9.98 us  [exchange(): lax.all_to_all(block, 'order', split_axis=0, concat_axis=0, tiled=True)]
    all_to_all x1, blocking collectives: 22.1 us -> 17.9 us  [exchange(): lax.all_to_all(block, 'order', split_axis=0, concat_axis=0, tiled=True)]
    ppermute x4 -> x2, waiting for transfers between devices: 6.21 us -> 2.16 us  [shift(): lax.ppermute(block, 'axial', [(i, (i + offset) % count) for i in range(co...]
    all_to_all x2, starting transfers between devices: 13 us -> 17 us  [exchange(): lax.all_to_all(block, 'order', split_axis=0, concat_axis=0, tiled=True)]
    ppermute x4 -> x2, starting transfers between devices: 9.32 us -> 6.48 us  [shift(): lax.ppermute(block, 'axial', [(i, (i + offset) % count) for i in range(co...]
    pallas_call x1, Pallas kernels: 2.22 us -> 4.22 us  [axial_stage(): call(functools.partial(axial_kernel, groups, band, step), 'axial_stage',...]
  transfers between devices with their start and end apart: 6 -> 4, of which waited for: 2 -> 2; matrix products, arithmetic and copies ran while one was open for 0% -> 0% of each run, Pallas kernels for 15% -> 19%
where the time goes in v1:
time: 81.4 us; the launch traced here: 81 us
  Pallas kernels  27.2 us (33%)
  starting transfers between devices  23.5 us (29%)
  blocking collectives  17.9 us (22%)
  waiting for transfers between devices  12.1 us (15%)
    all_to_all x1, blocking collectives, exchange(): lax.all_to_all(block, 'order', split_axis=0, concat_axis=0, tiled=True)  17.9 us
    all_to_all x2, starting transfers between devices, exchange(): lax.all_to_all(block, 'order', split_axis=0, concat_axis=0, tiled=True)  17 us
    all_to_all x2, waiting for transfers between devices, exchange(): lax.all_to_all(block, 'order', split_axis=0, concat_axis=0, tiled=True)  9.98 us
    pallas_call x1, Pallas kernels, physical_stage(): call(functools.partial(physical_kernel, groups, band, step, math.sqrt(2.0...  7.62 us
    ppermute x2, starting transfers between devices, shift(): lax.ppermute(block, 'axial', [(i, (i + offset) % count) for i in range(co...  6.48 us
    pallas_call x1, Pallas kernels, azimuthal_table(): call(functools.partial(table_kernel, slots), 'azimuthal_table', pltpu.HBM...  5.05 us
    pallas_call x1, Pallas kernels, axial_stage(): call(functools.partial(axial_kernel, groups, band, step), 'axial_stage',...  4.22 us
    pallas_call x1, Pallas kernels, radial_raw(): call(raw_kernel, 'radial_raw', (pltpu.HBM((R, rows), BF16), jax.ShapeDtyp...  3.98 us
  transfers between devices with their start and end apart: 4, of which 2 were waited for; matrix products, arithmetic and copies ran while one was open for 0% of the time, Pallas kernels for 19%

profile of v1, /device:TPU:1, one launch (start us, length us, event | category | flops | bytes accessed | tf_op | source)
XLA Modules:
  0.0 81.0 jit_solution(16464703408169841195)
XLA Ops:
  0.0 1.3 %stage.1.x_ref = bf16[3,2,32,2,1024]{4,3,2,1,0:T(2,128)(2,1)S(1)} custom-call(bf16[4,2,32,2,1024]{4,3,2,1,0:T(2,128)(2,1)} %x_far.1), custom_call_target="tpu_custom_call" | custom-call | tf_op jit(solution)/shard_map/stage/pallas_call | solution.py:88
  1.3 0.0 copy-start.5
  1.3 6.5 %collective-permute-start.1 = (bf16[3,2,32,2,1024]{4,3,2,1,0:T(2,128)(2,1)S(1)}, bf16[3,2,32,2,1024]{4,3,2,1,0:T(2,128)(2,1)S(1)}, u32[]{:S(2)}, u32[]{:S(2)}) collective-permute-start(bf16[3,2,32,2,1024]{4,3,2,1,0:T(2,128)(2,1)S(1)} %stage.1.x_ref), channel_id=1, source_target_pairs={{0,7},{1,0},{2,1},{3,2},{4,3},{5,4},{6,5},{7,6},{8,15},{9,8},{10,9... | collective-permute-start | bytes 2359304 | tf_op jit(solution)/shard_map/ppermute | solution.py:376
  7.8 0.0 collective-permute-start
  7.8 4.0 %radial_raw.1 = (bf16[1024,128]{1,0:T(8,128)(2,1)}, s32[128,128]{1,0:T(8,128)S(1)}, f32[128,128]{1,0:T(8,128)S(1)}) custom-call(s32[8,128]{1,0:T(8,128)} %bitcast.12, s32[8,128]{1,0:T(8,128)} %bitcast.16, bf16[4,2,32,2,1024]{4,3,2,1,0:T(2,128)(2,1)} %x_far.1, bf16[1024,1024]{1,0:T(8,128)(2,1)} %constant.10.clone.table_far.table_ref), custom_call_target="tpu_custom_call" | custom-call | tf_op jit(solution)/shard_map/radial_raw/pallas_call | solution.py:170
  11.7 8.0 %all-to-all-start.1 = ((bf16[32,32,128]{2,1,0:T(8,128)(2,1)}), bf16[32,32,128]{2,1,0:T(8,128)(2,1)S(1)}, u32[]{:S(2)}, u32[]{:S(2)}) async-start(bf16[32,32,128]{2,1,0:T(8,128)(2,1)} %bitcast.15), calls=%async_computation.1 | async-start | bytes 524288 | tf_op jit(solution)/shard_map/all_to_all | solution.py:380
  19.8 0.0 copy-done.5
  19.8 0.0 copy-start
  19.8 0.0 copy-start.3
  19.8 5.0 %azimuthal_table.1.far_ref = bf16[2048,2048]{1,0:T(8,128)(2,1)} custom-call(s32[8,128]{1,0:T(8,128)S(1)} %bitcast.13), custom_call_target="tpu_custom_call" | custom-call | tf_op jit(solution)/shard_map/azimuthal_table/pallas_call | solution.py:246
  24.9 0.0 collective-permute-done.1.high_ref
  24.9 2.2 %collective-permute-done.low_ref = bf16[3,2,32,2,1024]{4,3,2,1,0:T(2,128)(2,1)S(1)} collective-permute-done((bf16[3,2,32,2,1024]{4,3,2,1,0:T(2,128)(2,1)S(1)}, bf16[3,2,32,2,1024]{4,3,2,1,0:T(2,128)(2,1)S(1)}, u32[]{:S(2)}, u32[]{:S(2)}) %collective-permute-start) | collective-permute-done | bytes 786464 | tf_op jit(solution)/shard_map/ppermute | solution.py:376
  27.1 0.0 copy-done
  27.1 0.0 copy-done.3
  27.1 0.0 copy-start.2
  27.1 2.5 %radial_slope.1 = bf16[1024,384]{1,0:T(8,128)(2,1)} custom-call(bf16[3,2,32,2,1024]{4,3,2,1,0:T(2,128)(2,1)S(1)} %stage.1.x_ref, bf16[3,2,32,2,1024]{4,3,2,1,0:T(2,128)(2,1)S(1)} %collective-permute-done.low_ref, bf16[3,2,32,2,1024]{4,3,2,1,0:T(2,128)(2,1)S(1)} %collective-permute-done.1.high_ref, s32[128,128]{1,0:T(8,128)S(1)} %get-tuple-element.11.lens_ref, ...), custom_call_target="tpu_custom_call" | custom-call | tf_op jit(solution)/shard_map/radial_slope/pallas_call | solution.py:198
  29.6 0.0 all-to-all-done.1
  29.6 9.0 %all-to-all-start = ((bf16[32,32,384]{2,1,0:T(8,128)(2,1)}), bf16[32,32,384]{2,1,0:T(8,128)(2,1)S(1)}, u32[]{:S(2)}, u32[]{:S(2)}) async-start(bf16[32,32,384]{2,1,0:T(8,128)(2,1)} %bitcast.14), calls=%async_computation | async-start | bytes 1572864 | tf_op jit(solution)/shard_map/all_to_all | solution.py:380
  38.5 0.0 copy-done.2
  38.5 4.2 %axial_stage.1.axial_ref = f32[64,2048]{1,0:T(8,128)S(1)} custom-call(bf16[1024,128]{1,0:T(8,128)(2,1)S(1)} %bitcast.11, bf16[128,256]{1,0:T(8,128)(2,1)S(1)} %copy-done.2, bf16[2048,2048]{1,0:T(8,128)(2,1)} %azimuthal_table.1.far_ref), custom_call_target="tpu_custom_call" | custom-call | tf_op jit(solution)/shard_map/axial_stage/pallas_call | solution.py:292
  42.8 10.0 %all-to-all-done = bf16[32,32,384]{2,1,0:T(8,128)(2,1)S(1)} async-done(((bf16[32,32,384]{2,1,0:T(8,128)(2,1)}), bf16[32,32,384]{2,1,0:T(8,128)(2,1)S(1)}, u32[]{:S(2)}, u32[]{:S(2)}) %all-to-all-start) | async-done | bytes 786464 | tf_op jit(solution)/shard_map/all_to_all | solution.py:380
  52.8 0.0 copy-start.1
  52.8 0.0 copy-start.4
  52.8 7.6 %physical_stage.1 = bf16[1024,384]{1,0:T(8,128)(2,1)S(1)} custom-call(bf16[1024,384]{1,0:T(8,128)(2,1)S(1)} %bitcast.8, f32[64,2048]{1,0:T(8,128)S(1)} %axial_stage.1.axial_ref, bf16[128,256]{1,0:T(8,128)(2,1)S(1)} %copy-done.2, bf16[2048,2048]{1,0:T(8,128)(2,1)} %azimuthal_table.1.far_ref), custom_call_target="tpu_custom_call" | custom-call | tf_op jit(solution)/shard_map/physical_stage/pallas_call | solution.py:341
  60.4 17.9 %all_to_all.33 = bf16[32,32,384]{2,1,0:T(8,128)(2,1)S(1)} all-to-all(bf16[32,32,384]{2,1,0:T(8,128)(2,1)S(1)} %bitcast.9), channel_id=1, replica_groups=mesh['order'=32,'axial'=8] {'order'}, dimensions={0} | all-to-all | bytes 1572864 | tf_op jit(solution)/shard_map/all_to_all | solution.py:380
  78.2 0.0 copy-done.1
  78.2 0.0 copy-done.4
  78.2 2.6 %radial_analysis.1 = bf16[3,2,32,2,1024]{4,3,2,1,0:T(2,128)(2,1)} custom-call(bf16[1024,384]{1,0:T(8,128)(2,1)S(1)} %bitcast.10, s32[128,128]{1,0:T(8,128)S(1)} %get-tuple-element.11.lens_ref, bf16[128,128]{1,0:T(8,128)(2,1)S(1)} %copy-done.4, bf16[1024,1024]{1,0:T(8,128)(2,1)S(1)} %copy-done.1), custom_call_target="tpu_custom_call" | custom-call | tf_op jit(solution)/shard_map/radial_analysis/pallas_call | solution.py:368
Async XLA Ops:
  1.3 18.5 %copy-start.5 = (s32[1024]{0:T(1024)S(1)}, s32[1024]{0:T(1024)}, u32[]{:S(2)}) copy-start(s32[1024]{0:T(1024)} %param.9) | copy-start | bytes 12292
  1.3 23.6 %collective-permute-start.1 = (bf16[3,2,32,2,1024]{4,3,2,1,0:T(2,128)(2,1)S(1)}, bf16[3,2,32,2,1024]{4,3,2,1,0:T(2,128)(2,1)S(1)}, u32[]{:S(2)}, u32[]{:S(2)}) collective-permute-start(bf16[3,2,32,2,1024]{4,3,2,1,0:T(2,128)(2,1)S(1)} %stage.1.x_ref), channel_id=1, source_target_pairs={{0,7},{1,0},{2,1},{3,2},{4,3},{5,4},{6,5},{7,6},{8,15},{9,8},{10,9... | collective-permute-start | bytes 2359304 | tf_op jit(solution)/shard_map/ppermute | solution.py:376
  7.8 19.3 %collective-permute-start = (bf16[3,2,32,2,1024]{4,3,2,1,0:T(2,128)(2,1)S(1)}, bf16[3,2,32,2,1024]{4,3,2,1,0:T(2,128)(2,1)S(1)}, u32[]{:S(2)}, u32[]{:S(2)}) collective-permute-start(bf16[3,2,32,2,1024]{4,3,2,1,0:T(2,128)(2,1)S(1)} %stage.1.x_ref), channel_id=1, source_target_pairs={{0,1},{1,2},{2,3},{3,4},{4,5},{5,6},{6,7},{7,0},{8,9},{9,10},{10,1... | collective-permute-start | bytes 2359304 | tf_op jit(solution)/shard_map/ppermute | solution.py:376
  11.7 17.8 %all-to-all-start.1 = ((bf16[32,32,128]{2,1,0:T(8,128)(2,1)}), bf16[32,32,128]{2,1,0:T(8,128)(2,1)S(1)}, u32[]{:S(2)}, u32[]{:S(2)}) async-start(bf16[32,32,128]{2,1,0:T(8,128)(2,1)} %bitcast.15), calls=%async_computation.1 | async-start | bytes 524288 | tf_op jit(solution)/shard_map/all_to_all | solution.py:380
  19.8 7.3 %copy-start = (bf16[1024,1024]{1,0:T(8,128)(2,1)S(1)}, bf16[1024,1024]{1,0:T(8,128)(2,1)}, u32[]{:S(2)}) copy-start(bf16[1024,1024]{1,0:T(8,128)(2,1)} %constant.10.clone.table_far.table_ref) | copy-start | bytes 6291460
  19.8 7.2 %copy-start.3 = (bf16[128,384]{1,0:T(8,128)(2,1)S(1)}, bf16[128,384]{1,0:T(8,128)(2,1)}, u32[]{:S(2)}) copy-start(bf16[128,384]{1,0:T(8,128)(2,1)} %constant.11.clone.rows_ref) | copy-start | bytes 294916
  27.1 11.5 %copy-start.2 = (bf16[128,256]{1,0:T(8,128)(2,1)S(1)}, bf16[128,256]{1,0:T(8,128)(2,1)}, u32[]{:S(2)}) copy-start(bf16[128,256]{1,0:T(8,128)(2,1)} %constant.12.clone.both_ref) | copy-start | bytes 196612
  29.6 23.2 %all-to-all-start = ((bf16[32,32,384]{2,1,0:T(8,128)(2,1)}), bf16[32,32,384]{2,1,0:T(8,128)(2,1)S(1)}, u32[]{:S(2)}, u32[]{:S(2)}) async-start(bf16[32,32,384]{2,1,0:T(8,128)(2,1)} %bitcast.14), calls=%async_computation | async-start | bytes 1572864 | tf_op jit(solution)/shard_map/all_to_all | solution.py:380
  52.8 25.5 %copy-start.1 = (bf16[1024,1024]{1,0:T(8,128)(2,1)S(1)}, bf16[1024,1024]{1,0:T(8,128)(2,1)}, u32[]{:S(2)}) copy-start(bf16[1024,1024]{1,0:T(8,128)(2,1)} %constant.14.clone.table_ref) | copy-start | bytes 6291460
  52.8 25.5 %copy-start.4 = (bf16[128,128]{1,0:T(8,128)(2,1)S(1)}, bf16[128,128]{1,0:T(8,128)(2,1)}, u32[]{:S(2)}) copy-start(bf16[128,128]{1,0:T(8,128)(2,1)} %constant.13.clone.back_ref) | copy-start | bytes 98308

commit v2 on v1

--- a/solution.py
+++ b/solution.py
@@ -26,23 +26,16 @@
 
 def plane_matrices(slots):
     width = 2 * slots * 2
-    pair = width // 2
-    inner = np.arange(width)
-    plane, rest = inner % 2, inner // 2
-    gather = np.zeros((width, width), np.float32)
-    gather[inner, plane * pair + rest] = 1.0
-    eye = np.eye(pair, dtype=np.float32)
+    eye = np.eye(width // 2, dtype=np.float32)
     own = np.kron(eye, np.array([[0, 8], [-8, 0]], np.float32))
     low = np.kron(eye, np.array([[1, -8], [0, 1]], np.float32))
     high = np.kron(eye, np.array([[-1, 0], [8, -1]], np.float32))
     rows = np.concatenate([own, low, high], axis=1)
-    swap = np.roll(np.eye(width, dtype=np.float32), pair, axis=1)
-    both = np.concatenate([gather, gather @ swap], axis=1)
-    return (
-        rows.astype(jnp.bfloat16),
-        both.astype(jnp.bfloat16),
-        gather.T.astype(jnp.bfloat16),
-    )
+    per = 128 // slots
+    source = np.arange(per * width).reshape(per, 2, slots, 2).transpose(3, 1, 0, 2).reshape(-1)
+    permutation = np.zeros((per * width, per * width), np.float32)
+    permutation[source, np.arange(per * width)] = 1.0
+    return rows.astype(jnp.bfloat16), permutation.astype(jnp.bfloat16)
 
 
 def dot(a, b, dims):
@@ -216,146 +209,176 @@
 
 
 def table_kernel(slots, orders_ref, far_ref, out_ref, sem):
-    points = out_ref.shape[1]
+    half = 128 * orders_ref.shape[0]
+    points = 2 * half
+    lane = lax.broadcasted_iota(jnp.int32, (slots, 128), 1)
     copies = []
-    lane = lax.broadcasted_iota(jnp.int32, (slots, 128), 1)
-    per_row = 128 // slots
     for row in range(orders_ref.shape[0]):
         column = jnp.broadcast_to(orders_ref[row:row + 1, :], (128, 128)).T
-        for piece in range(per_row):
+        for piece in range(128 // slots):
             orders = column[piece * slots:(piece + 1) * slots]
-            start = (row * per_row + piece) * 2 * slots
+            rows = pl.ds(row * 128 + piece * slots, slots)
             cos_now, sin_now = sine_cosine((orders * lane) & (points - 1), points)
             cos_turn, sin_turn = sine_cosine((orders * 128) & (points - 1), points)
-            for block in range(points // 128):
-                part = pl.ds(block * 128, 128)
-                out_ref[start:start + slots, part] = cos_now.astype(BF16)
-                out_ref[start + slots:start + 2 * slots, part] = (-sin_now).astype(BF16)
+            for block in range(half // 128):
+                out_ref[rows, pl.ds(block * 128, 128)] = cos_now.astype(BF16)
+                out_ref[rows, pl.ds(half + (block + 1) * 128, 128)] = (-sin_now).astype(BF16)
                 cos_now, sin_now = (
                     cos_now * cos_turn - sin_now * sin_turn,
                     sin_now * cos_turn + cos_now * sin_turn,
                 )
-        part = pl.ds(row * 256, 256)
+            sign = jnp.where(lane == 0, 1 - 2 * (orders & 1), 0)
+            out_ref[rows, pl.ds(half, 128)] = sign.astype(F32).astype(BF16)
+        part = pl.ds(row * 128, 128)
         copies.append(pltpu.make_async_copy(out_ref.at[part], far_ref.at[part], sem.at[row]))
         copies[-1].start()
     for copy in copies:
         copy.wait()
 
 
-def azimuthal_table(orders, slots, points):
+def azimuthal_table(orders, slots):
+    shape = (orders.size, 2 * orders.size + 128)
     return call(
         functools.partial(table_kernel, slots), "azimuthal_table",
-        pltpu.HBM((2 * orders.size, points), BF16), [HERE], FAR,
-        [pltpu.VMEM((2 * orders.size, points), BF16),
-         pltpu.SemaphoreType.DMA((orders.shape[0],))],
+        pltpu.HBM(shape, BF16), [HERE], FAR,
+        [pltpu.VMEM(shape, BF16), pltpu.SemaphoreType.DMA((orders.shape[0],))],
     )(orders)
 
 
-def place_field(lhs, mapped, row, groups, band):
-    width = mapped.shape[1] // 2
-    low_lanes = lax.broadcasted_iota(jnp.int32, (band, width), 1) < width // 2
-    for pair in range(groups // 2):
-        even = mapped[2 * pair * band:(2 * pair + 1) * band]
-        odd = mapped[(2 * pair + 1) * band:(2 * pair + 2) * band]
-        first = jnp.where(low_lanes, even[:, :width], odd[:, width:])
-        second = jnp.where(low_lanes, even[:, width:], odd[:, :width])
-        cols = pl.ds(pair * width, width)
-        lhs[row:row + band, cols] = first.astype(BF16)
-        lhs[row + band:row + 2 * band, cols] = second.astype(BF16)
-
-
-def table_loads(far_ref, table_ref, sem, step):
-    rows, points = table_ref.shape
+def place_field(lhs, row, bands, perm_ref, groups, band):
+    per = perm_ref.shape[0] // bands.shape[1]
+    stacked = jnp.concatenate([
+        jnp.concatenate(
+            [bands[(tile * per + e) * band:(tile * per + e + 1) * band] for e in range(per)], axis=1
+        )
+        for tile in range(groups // per)
+    ], axis=0)
+    mapped = dot(stacked, perm_ref[...], ((1,), (0,))).astype(BF16)
+    for tile in range(groups // per):
+        for plane in range(2):
+            for part in range(2):
+                lanes = (2 * plane + part) * 128
+                lhs[part, row + plane * band:row + (plane + 1) * band,
+                    pl.ds(tile * 128, 128)] = mapped[tile * band:(tile + 1) * band,
+                                                     lanes:lanes + 128]
+
+
+def table_loads(far_ref, table_ref, sem):
+    rows, columns = table_ref.shape
+    half = rows
+    step = half // 2
+    pieces = [(0, step), (half + 128, step), (step, step + 128), (half + 128 + step, step)]
     loads = []
-    for block in range(points // step):
+    for start, size in pieces:
         loads.append([])
         for piece in range(4):
-            area = (pl.ds(piece * (rows // 4), rows // 4), pl.ds(block * step, step))
+            area = (pl.ds(piece * (rows // 4), rows // 4), pl.ds(start, size))
+            index = 4 * (len(loads) - 1) + piece
             loads[-1].append(pltpu.make_async_copy(
-                far_ref.at[area], table_ref.at[area], sem.at[4 * block + piece]))
+                far_ref.at[area], table_ref.at[area], sem.at[index]))
             loads[-1][-1].start()
-    return loads
-
-
-def axial_kernel(groups, band, step, raw_ref, both_ref, far_ref, axial_ref, lhs, table_ref, sem):
-    loads = table_loads(far_ref, table_ref, sem, step)
-    place_field(lhs, dot(raw_ref[...], both_ref[...], ((1,), (0,))), 0, groups, band)
-    for block in range(table_ref.shape[1] // step):
-        part = pl.ds(block * step, step)
-        for load in loads[block]:
+    return pieces, loads
+
+
+def axial_kernel(groups, band, raw_ref, perm_ref, far_ref, axial_ref, lhs, table_ref, sem):
+    pieces, loads = table_loads(far_ref, table_ref, sem)
+    place_field(lhs, 0, raw_ref[...], perm_ref, groups, band)
+    half = table_ref.shape[0]
+    for index, (start, size) in enumerate(pieces):
+        for load in loads[index]:
             load.wait()
-        axial_ref[:, part] = dot(lhs[...], table_ref[:, part], ((1,), (0,))) * (1.0 / 12.0)
-
-
-def axial_stage(raw, both, table, groups, band, step=512):
-    rows, points = table.shape
-    return call(
-        functools.partial(axial_kernel, groups, band, step), "axial_stage",
-        jax.ShapeDtypeStruct((2 * band, points), F32),
+        part = pl.ds(start, size)
+        values = dot(lhs[index % 2], table_ref[:, part], ((1,), (0,)))
+        column = lax.broadcasted_iota(jnp.int32, values.shape, 1) + start
+        once = (column == 0) | (column == half)
+        axial_ref[:, part] = values * jnp.where(once, 1.0 / 12.0, 1.0 / 6.0)
+
+
+def axial_stage(raw, perm, table, groups, band):
+    rows, columns = table.shape
+    return call(
+        functools.partial(axial_kernel, groups, band), "axial_stage",
+        jax.ShapeDtypeStruct((2 * band, columns), F32),
         [HERE, HERE, FAR], HERE,
-        [pltpu.VMEM((2 * band, rows), BF16), pltpu.VMEM(table.shape, BF16),
-         pltpu.SemaphoreType.DMA((4 * (points // step),))],
-        limit=20,
-    )(raw, both, in_hbm(table))
-
-
-def physical_kernel(groups, band, step, scale, slope_ref, axial_ref, both_ref, far_ref, out_ref,
-                    lhs, products, table_ref, sem):
-    width = both_ref.shape[0]
-    half = width // 2
-    rows, points = table_ref.shape
-    loads = table_loads(far_ref, table_ref, sem, step)
+        [pltpu.VMEM((2, 2 * band, rows), BF16), pltpu.VMEM(table.shape, BF16),
+         pltpu.SemaphoreType.DMA((16,))],
+    )(raw, perm, in_hbm(table))
+
+
+def physical_kernel(groups, band, step, scale, slope_ref, axial_ref, perm_ref, far_ref, out_ref,
+                    lhs, even, odd, table_ref, sem):
+    pieces, loads = table_loads(far_ref, table_ref, sem)
+    width = slope_ref.shape[1] // 3
+    half = table_ref.shape[0]
+    per = perm_ref.shape[0] // width
     for field in range(3):
-        mapped = dot(slope_ref[:, field * width:(field + 1) * width], both_ref[...], ((1,), (0,)))
-        place_field(lhs, mapped, 2 * field * band, groups, band)
-    for block in range(points // step):
-        part = pl.ds(block * step, step)
-        for load in loads[block]:
+        place_field(lhs, 2 * field * band, slope_ref[:, field * width:(field + 1) * width],
+                    perm_ref, groups, band)
+    for index in (0, 2):
+        (start, size), (other, span) = pieces[index], pieces[index + 1]
+        for load in loads[index]:
             load.wait()
-        values = dot(lhs[...], table_ref[:, part], ((1,), (0,)))
-        axial = axial_ref[:, part]
+        cosines = dot(lhs[0], table_ref[:, pl.ds(start, size)], ((1,), (0,)))
+        for load in loads[index + 1]:
+            load.wait()
+        sines = dot(lhs[1], table_ref[:, pl.ds(other, span)], ((1,), (0,)))
+        axial_cos = axial_ref[:, pl.ds(start, size)]
+        axial_sin = axial_ref[:, pl.ds(other, span)]
         for g in range(3):
             area = slice(2 * g * band, (2 * g + 2) * band)
-            products[area, part] = (values[area] * axial).astype(BF16)
-
-    low_lanes = lax.broadcasted_iota(jnp.int32, (band, width), 1) < half
-    for start in range(0, rows, step):
-        part = pl.ds(start, step)
-        spectral = dot(products[...], table_ref[part, :], ((1,), (1,))) * scale
+            c, s = cosines[area], sines[area]
+            part = pl.ds(start, span)
+            even[area, part] = (c[:, :span] * axial_cos[:, :span] + s * axial_sin).astype(BF16)
+            odd[area, part] = (c[:, :span] * axial_sin + s * axial_cos[:, :span]).astype(BF16)
+            if size > span:
+                edge = (c[:, span:] * axial_cos[:, span:]).astype(BF16)
+                even[area, pl.ds(start + span, size - span)] = edge
+
+    for start in range(0, half, step):
+        rows = pl.ds(start, step)
+        parts = [
+            (dot(even[...], table_ref[rows, 0:half + 128], ((1,), (1,))) * scale).astype(BF16),
+            (dot(odd[...], table_ref[rows, half + 128:], ((1,), (1,))) * scale).astype(BF16),
+        ]
+        stacked = jnp.concatenate([
+            jnp.concatenate([
+                parts[part][(2 * g + plane) * band:(2 * g + plane + 1) * band,
+                            tile * 128:(tile + 1) * 128]
+                for plane in range(2) for part in range(2)
+            ], axis=1)
+            for g in range(3) for tile in range(step // 128)
+        ], axis=0)
+        mapped = dot(stacked, perm_ref[...], ((1,), (1,))).astype(BF16)
         for g in range(3):
-            out_cols = pl.ds(g * width, width)
-            for tile in range(step // width):
-                cols = slice(tile * width, (tile + 1) * width)
-                first = spectral[(2 * g) * band:(2 * g + 1) * band, cols]
-                second = spectral[(2 * g + 1) * band:(2 * g + 2) * band, cols]
-                even = jnp.where(low_lanes, first, pltpu.roll(second, half, 1))
-                odd = jnp.where(low_lanes, pltpu.roll(first, half, 1), second)
-                row = (start // width + tile) * 2 * band
-                out_ref[row:row + band, out_cols] = even.astype(BF16)
-                out_ref[row + band:row + 2 * band, out_cols] = odd.astype(BF16)
-
-
-def physical_stage(slope, axial, both, table, groups, band, step=512):
-    rows, points = table.shape
-    width = both.shape[0]
-    return call(
-        functools.partial(physical_kernel, groups, band, step, math.sqrt(2.0 / points)),
-        "physical_stage",
-        jax.ShapeDtypeStruct((groups * band, 3 * width), BF16), [HERE] * 3 + [FAR], HERE,
-        [pltpu.VMEM((6 * band, rows), BF16), pltpu.VMEM((6 * band, points), BF16),
-         pltpu.VMEM(table.shape, BF16), pltpu.SemaphoreType.DMA((4 * (points // step),))],
+            for tile in range(step // 128):
+                source = (g * (step // 128) + tile) * band
+                for e in range(per):
+                    row = ((start // 128 + tile) * per + e) * band
+                    out_ref[row:row + band, pl.ds(g * width, width)] = mapped[
+                        source:source + band, e * width:(e + 1) * width]
+
+
+def physical_stage(slope, axial, perm, table, groups, band, step=512):
+    rows = table.shape[0]
+    scale = math.sqrt(1.0 / rows)
+    return call(
+        functools.partial(physical_kernel, groups, band, step, scale), "physical_stage",
+        jax.ShapeDtypeStruct(slope.shape, BF16), [HERE] * 3 + [FAR], HERE,
+        [pltpu.VMEM((2, 6 * band, rows), BF16), pltpu.VMEM((6 * band, rows + 128), BF16),
+         pltpu.VMEM((6 * band, rows), BF16), pltpu.VMEM(table.shape, BF16),
+         pltpu.SemaphoreType.DMA((16,))],
         limit=28,
-    )(slope, axial, both, in_hbm(table))
-
-
-def final_kernel(x_ref, lens_ref, back_ref, table_ref, out_ref, buffer, sem):
-    width = back_ref.shape[0]
+    )(slope, axial, perm, in_hbm(table))
+
+
+def final_kernel(x_ref, lens_ref, table_ref, out_ref, buffer, sem):
+    width = x_ref.shape[1] // 3
     modes = lax.broadcasted_iota(jnp.int32, (width, table_ref.shape[1]), 1)
     keep = modes < lens_ref[:, :1]
     copies = []
     for g in range(3):
-        mapped = dot(x_ref[:, g * width:(g + 1) * width], back_ref[...], ((1,), (0,)))
-        result = dot(mapped.astype(BF16), table_ref[...], ((0,), (0,)))
+        part = x_ref[:, g * width:(g + 1) * width]
+        result = dot(part, table_ref[...], ((0,), (0,)))
         rows = jnp.where(keep, result, 0.0).astype(BF16)
         buffer[g] = rows.reshape(buffer.shape[1:])
         copies.append(pltpu.make_async_copy(buffer.at[g], out_ref.at[g], sem.at[g]))
@@ -364,11 +387,11 @@
         copy.wait()
 
 
-def radial_analysis(x, lens, back, table, shape):
-    return call(
-        final_kernel, "radial_analysis", pltpu.HBM(shape, BF16), [HERE] * 4, FAR,
+def radial_analysis(x, lens, table, shape):
+    return call(
+        final_kernel, "radial_analysis", pltpu.HBM(shape, BF16), [HERE] * 3, FAR,
         [pltpu.VMEM(shape, BF16), pltpu.SemaphoreType.DMA((3,))],
-    )(x, lens, back, table)
+    )(x, lens, table)
 
 
 def shift(block, offset):
@@ -383,12 +406,11 @@
 def shards(coefficients, order_lists, lengths):
     field_count, part_count, slots, planes, modes = coefficients.shape
     order_count = order_lists.shape[0]
-    points = 2 * order_count
     groups = lax.axis_size("order")
     band = R // groups
     width = part_count * slots * planes
     synthesis, analysis = radial_constants(R, modes)
-    rows_map, both, back = plane_matrices(slots)
+    rows_map, perm = plane_matrices(slots)
 
     sloped = stage(coefficients)
     low, high = shift(sloped, 1), shift(sloped, -1)
@@ -397,15 +419,15 @@
         orders, lengths.reshape(order_count // 128, 128), coefficients, synthesis
     )
     raw_bands = exchange(bands)
-    table = azimuthal_table(orders, slots, points)
+    table = azimuthal_table(orders, slots)
     later_lens, table = lax.optimization_barrier((lens, table))
     slope_bands = exchange(
         radial_slope(sloped, low, high, later_lens, weight, rows_map, synthesis)
     )
-    axial = axial_stage(raw_bands, both, table, groups, band)
-    spectral = physical_stage(slope_bands, axial, both, table, groups, band)
+    axial = axial_stage(raw_bands, perm, table, groups, band)
+    spectral = physical_stage(slope_bands, axial, perm, table, groups, band)
     shape = (3, part_count, slots, planes, modes)
-    return radial_analysis(exchange(spectral), lens, back, analysis, shape)
+    return radial_analysis(exchange(spectral), lens, analysis, shape)
 
 
 def solution(mesh):

time: 81.4 us -> 80.3 us (0.986)
  Pallas kernels: 27.2 us -> 21.2 us
  waiting for transfers between devices: 12.1 us -> 15.2 us
  local copies, waits for them, and re-layouts: 0.03 us -> 2.04 us
    pallas_call x3, Pallas kernels: 14.4 us -> 9.99 us  [the longest x1 5.39 us: physical_stage(): call(functools.partial(physical_kernel, groups, band, step, scale), 'phys...]
    unnamed x12 -> x14, local copies, waits for them, and re-layouts: 0.03 us -> 2.04 us
    ppermute x2, waiting for transfers between devices: 2.16 us -> 3.72 us  [shift(): lax.ppermute(block, 'axial', [(i, (i + offset) % count) for i in range(co...]
    pallas_call x1, Pallas kernels: 5.05 us -> 3.51 us  [azimuthal_table(): call(functools.partial(table_kernel, slots), 'azimuthal_table', pltpu.HBM...]
    all_to_all x2, waiting for transfers between devices: 9.98 us -> 11.5 us  [exchange(): lax.all_to_all(block, 'order', split_axis=0, concat_axis=0, tiled=True)]
  transfers between devices with their start and end apart: 4 -> 4, of which waited for: 2 -> 3; matrix products, arithmetic and copies ran while one was open for 0% -> 0% of each run, Pallas kernels for 19% -> 16%
where the time goes in v2:
time: 80.3 us; the launch traced here: 79.9 us
  starting transfers between devices  23.5 us (29%)
  Pallas kernels  21.2 us (26%)
  blocking collectives  17.9 us (22%)
  waiting for transfers between devices  15.2 us (19%)
  local copies, waits for them, and re-layouts  2.04 us (3%)
    all_to_all x1, blocking collectives, exchange(): lax.all_to_all(block, 'order', split_axis=0, concat_axis=0, tiled=True)  17.9 us
    all_to_all x2, starting transfers between devices, exchange(): lax.all_to_all(block, 'order', split_axis=0, concat_axis=0, tiled=True)  17 us
    all_to_all x2, waiting for transfers between devices, exchange(): lax.all_to_all(block, 'order', split_axis=0, concat_axis=0, tiled=True)  11.5 us
    ppermute x2, starting transfers between devices, shift(): lax.ppermute(block, 'axial', [(i, (i + offset) % count) for i in range(co...  6.48 us
    pallas_call x1, Pallas kernels, physical_stage(): call(functools.partial(physical_kernel, groups, band, step, scale), 'phys...  5.39 us
    pallas_call x1, Pallas kernels, radial_raw(): call(raw_kernel, 'radial_raw', (pltpu.HBM((R, rows), BF16), jax.ShapeDtyp...  3.96 us
    ppermute x2, waiting for transfers between devices, shift(): lax.ppermute(block, 'axial', [(i, (i + offset) % count) for i in range(co...  3.72 us
    pallas_call x1, Pallas kernels, azimuthal_table(): call(functools.partial(table_kernel, slots), 'azimuthal_table', pltpu.HBM...  3.51 us
  transfers between devices with their start and end apart: 4, of which 3 were waited for; matrix products, arithmetic and copies ran while one was open for 0% of the time, Pallas kernels for 16%

profile of v2, /device:TPU:1, one launch (start us, length us, event | category | flops | bytes accessed | tf_op | source)
XLA Modules:
  0.0 79.9 jit_solution(616370752391874727)
XLA Ops:
  0.0 1.3 %stage.1.x_ref = bf16[3,2,32,2,1024]{4,3,2,1,0:T(2,128)(2,1)S(1)} custom-call(bf16[4,2,32,2,1024]{4,3,2,1,0:T(2,128)(2,1)} %x_far.1), custom_call_target="tpu_custom_call" | custom-call | tf_op jit(solution)/shard_map/stage/pallas_call | solution.py:81
  1.3 0.0 copy-start.6
  1.3 6.5 %collective-permute-start.1 = (bf16[3,2,32,2,1024]{4,3,2,1,0:T(2,128)(2,1)S(1)}, bf16[3,2,32,2,1024]{4,3,2,1,0:T(2,128)(2,1)S(1)}, u32[]{:S(2)}, u32[]{:S(2)}) collective-permute-start(bf16[3,2,32,2,1024]{4,3,2,1,0:T(2,128)(2,1)S(1)} %stage.1.x_ref), channel_id=1, source_target_pairs={{0,7},{1,0},{2,1},{3,2},{4,3},{5,4},{6,5},{7,6},{8,15},{9,8},{10,9... | collective-permute-start | bytes 2359304 | tf_op jit(solution)/shard_map/ppermute | solution.py:399
  7.8 0.0 collective-permute-start
  7.8 4.0 %radial_raw.1 = (bf16[1024,128]{1,0:T(8,128)(2,1)}, s32[128,128]{1,0:T(8,128)S(1)}, f32[128,128]{1,0:T(8,128)S(1)}) custom-call(s32[8,128]{1,0:T(8,128)} %bitcast.12, s32[8,128]{1,0:T(8,128)} %bitcast.16, bf16[4,2,32,2,1024]{4,3,2,1,0:T(2,128)(2,1)} %x_far.1, bf16[1024,1024]{1,0:T(8,128)(2,1)} %constant.8.clone.table_far.table_ref), custom_call_target="tpu_custom_call" | custom-call | tf_op jit(solution)/shard_map/radial_raw/pallas_call | solution.py:163
  11.7 8.0 %all-to-all-start.1 = ((bf16[32,32,128]{2,1,0:T(8,128)(2,1)}), bf16[32,32,128]{2,1,0:T(8,128)(2,1)S(1)}, u32[]{:S(2)}, u32[]{:S(2)}) async-start(bf16[32,32,128]{2,1,0:T(8,128)(2,1)} %bitcast.15), calls=%async_computation.1 | async-start | bytes 524288 | tf_op jit(solution)/shard_map/all_to_all | solution.py:403
  19.8 0.0 copy-done.6
  19.8 0.0 copy-start
  19.8 0.0 copy-start.5
  19.8 3.5 %azimuthal_table.1.far_ref = bf16[1024,2176]{1,0:T(8,128)(2,1)} custom-call(s32[8,128]{1,0:T(8,128)S(1)} %bitcast.13), custom_call_target="tpu_custom_call" | custom-call | tf_op jit(solution)/shard_map/azimuthal_table/pallas_call | solution.py:241
  23.3 0.6 collective-permute-done.1.high_ref
  24.0 3.1 %collective-permute-done.low_ref = bf16[3,2,32,2,1024]{4,3,2,1,0:T(2,128)(2,1)S(1)} collective-permute-done((bf16[3,2,32,2,1024]{4,3,2,1,0:T(2,128)(2,1)S(1)}, bf16[3,2,32,2,1024]{4,3,2,1,0:T(2,128)(2,1)S(1)}, u32[]{:S(2)}, u32[]{:S(2)}) %collective-permute-start) | collective-permute-done | bytes 786464 | tf_op jit(solution)/shard_map/ppermute | solution.py:399
  27.1 0.0 copy-start.3
  27.1 0.9 %copy-done.3 = bf16[3,2,32,2,1024]{4,3,2,1,0:T(2,128)(2,1)} copy-done((bf16[3,2,32,2,1024]{4,3,2,1,0:T(2,128)(2,1)}, bf16[3,2,32,2,1024]{4,3,2,1,0:T(2,128)(2,1)S(1)}, u32[]{:S(2)}) %copy-start.3) | copy-done | bytes 786456
  27.9 0.0 copy-done
  27.9 0.0 copy-done.5
  27.9 0.0 copy-start.4
  27.9 1.1 %copy-done.4 = bf16[3,2,32,2,1024]{4,3,2,1,0:T(2,128)(2,1)S(1)} copy-done((bf16[3,2,32,2,1024]{4,3,2,1,0:T(2,128)(2,1)S(1)}, bf16[3,2,32,2,1024]{4,3,2,1,0:T(2,128)(2,1)}, u32[]{:S(2)}) %copy-start.4) | copy-done | bytes 786456
  29.1 0.0 copy-start.2
  29.1 2.5 %radial_slope.1 = bf16[1024,384]{1,0:T(8,128)(2,1)} custom-call(bf16[3,2,32,2,1024]{4,3,2,1,0:T(2,128)(2,1)S(1)} %stage.1.x_ref, bf16[3,2,32,2,1024]{4,3,2,1,0:T(2,128)(2,1)S(1)} %copy-done.4, bf16[3,2,32,2,1024]{4,3,2,1,0:T(2,128)(2,1)S(1)} %collective-permute-done.1.high_ref, s32[128,128]{1,0:T(8,128)S(1)} %get-tuple-element.11.lens_ref, ...), custom_call_target="tpu_custom_call" | custom-call | tf_op jit(solution)/shard_map/radial_slope/pallas_call | solution.py:191
  31.6 0.0 all-to-all-done.1
  31.6 9.0 %all-to-all-start = ((bf16[32,32,384]{2,1,0:T(8,128)(2,1)}), bf16[32,32,384]{2,1,0:T(8,128)(2,1)S(1)}, u32[]{:S(2)}, u32[]{:S(2)}) async-start(bf16[32,32,384]{2,1,0:T(8,128)(2,1)} %bitcast.14), calls=%async_computation | async-start | bytes 1572864 | tf_op jit(solution)/shard_map/all_to_all | solution.py:403
  40.5 0.0 copy-done.2
  40.6 2.8 %axial_stage.1.axial_ref = f32[64,2176]{1,0:T(8,128)S(1)} custom-call(bf16[1024,128]{1,0:T(8,128)(2,1)S(1)} %bitcast.11, bf16[512,512]{1,0:T(8,128)(2,1)S(1)} %copy-done.2, bf16[1024,2176]{1,0:T(8,128)(2,1)} %azimuthal_table.1.far_ref), custom_call_target="tpu_custom_call" | custom-call | tf_op jit(solution)/shard_map/axial_stage/pallas_call | solution.py:299
  43.3 11.5 %all-to-all-done = bf16[32,32,384]{2,1,0:T(8,128)(2,1)S(1)} async-done(((bf16[32,32,384]{2,1,0:T(8,128)(2,1)}), bf16[32,32,384]{2,1,0:T(8,128)(2,1)S(1)}, u32[]{:S(2)}, u32[]{:S(2)}) %all-to-all-start) | async-done | bytes 786464 | tf_op jit(solution)/shard_map/all_to_all | solution.py:403
  54.8 0.0 copy-start.1
  54.8 5.4 %physical_stage.1 = bf16[1024,384]{1,0:T(8,128)(2,1)S(1)} custom-call(bf16[1024,384]{1,0:T(8,128)(2,1)S(1)} %bitcast.8, f32[64,2176]{1,0:T(8,128)S(1)} %axial_stage.1.axial_ref, bf16[512,512]{1,0:T(8,128)(2,1)S(1)} %copy-done.2, bf16[1024,2176]{1,0:T(8,128)(2,1)} %azimuthal_table.1.far_ref), custom_call_target="tpu_custom_call" | custom-call | tf_op jit(solution)/shard_map/physical_stage/pallas_call | solution.py:364
  60.2 17.9 %all_to_all.33 = bf16[32,32,384]{2,1,0:T(8,128)(2,1)S(1)} all-to-all(bf16[32,32,384]{2,1,0:T(8,128)(2,1)S(1)} %bitcast.9), channel_id=1, replica_groups=mesh['order'=32,'axial'=8] {'order'}, dimensions={0} | all-to-all | bytes 1572864 | tf_op jit(solution)/shard_map/all_to_all | solution.py:403
  78.0 0.0 copy-done.1
  78.0 1.8 %radial_analysis.1 = bf16[3,2,32,2,1024]{4,3,2,1,0:T(2,128)(2,1)} custom-call(bf16[1024,384]{1,0:T(8,128)(2,1)S(1)} %bitcast.10, s32[128,128]{1,0:T(8,128)S(1)} %get-tuple-element.11.lens_ref, bf16[1024,1024]{1,0:T(8,128)(2,1)S(1)} %copy-done.1), custom_call_target="tpu_custom_call" | custom-call | tf_op jit(solution)/shard_map/radial_analysis/pallas_call | solution.py:391
Async XLA Ops:
  1.3 18.5 %copy-start.6 = (s32[1024]{0:T(1024)S(1)}, s32[1024]{0:T(1024)}, u32[]{:S(2)}) copy-start(s32[1024]{0:T(1024)} %param.8) | copy-start | bytes 12292
  1.3 22.7 %collective-permute-start.1 = (bf16[3,2,32,2,1024]{4,3,2,1,0:T(2,128)(2,1)S(1)}, bf16[3,2,32,2,1024]{4,3,2,1,0:T(2,128)(2,1)S(1)}, u32[]{:S(2)}, u32[]{:S(2)}) collective-permute-start(bf16[3,2,32,2,1024]{4,3,2,1,0:T(2,128)(2,1)S(1)} %stage.1.x_ref), channel_id=1, source_target_pairs={{0,7},{1,0},{2,1},{3,2},{4,3},{5,4},{6,5},{7,6},{8,15},{9,8},{10,9... | collective-permute-start | bytes 2359304 | tf_op jit(solution)/shard_map/ppermute | solution.py:399
  7.8 19.3 %collective-permute-start = (bf16[3,2,32,2,1024]{4,3,2,1,0:T(2,128)(2,1)S(1)}, bf16[3,2,32,2,1024]{4,3,2,1,0:T(2,128)(2,1)S(1)}, u32[]{:S(2)}, u32[]{:S(2)}) collective-permute-start(bf16[3,2,32,2,1024]{4,3,2,1,0:T(2,128)(2,1)S(1)} %stage.1.x_ref), channel_id=1, source_target_pairs={{0,1},{1,2},{2,3},{3,4},{4,5},{5,6},{6,7},{7,0},{8,9},{9,10},{10,1... | collective-permute-start | bytes 2359304 | tf_op jit(solution)/shard_map/ppermute | solution.py:399
  11.7 19.8 %all-to-all-start.1 = ((bf16[32,32,128]{2,1,0:T(8,128)(2,1)}), bf16[32,32,128]{2,1,0:T(8,128)(2,1)S(1)}, u32[]{:S(2)}, u32[]{:S(2)}) async-start(bf16[32,32,128]{2,1,0:T(8,128)(2,1)} %bitcast.15), calls=%async_computation.1 | async-start | bytes 524288 | tf_op jit(solution)/shard_map/all_to_all | solution.py:403
  19.8 8.1 %copy-start = (bf16[1024,1024]{1,0:T(8,128)(2,1)S(1)}, bf16[1024,1024]{1,0:T(8,128)(2,1)}, u32[]{:S(2)}) copy-start(bf16[1024,1024]{1,0:T(8,128)(2,1)} %constant.8.clone.table_far.table_ref) | copy-start | bytes 6291460
  19.8 8.1 %copy-start.5 = (bf16[128,384]{1,0:T(8,128)(2,1)S(1)}, bf16[128,384]{1,0:T(8,128)(2,1)}, u32[]{:S(2)}) copy-start(bf16[128,384]{1,0:T(8,128)(2,1)} %constant.9.clone.rows_ref) | copy-start | bytes 294916
  27.1 0.9 %copy-start.3 = (bf16[3,2,32,2,1024]{4,3,2,1,0:T(2,128)(2,1)}, bf16[3,2,32,2,1024]{4,3,2,1,0:T(2,128)(2,1)S(1)}, u32[]{:S(2)}) copy-start(bf16[3,2,32,2,1024]{4,3,2,1,0:T(2,128)(2,1)S(1)} %collective-permute-done.low_ref) | copy-start | bytes 2359300
  27.9 1.1 %copy-start.4 = (bf16[3,2,32,2,1024]{4,3,2,1,0:T(2,128)(2,1)S(1)}, bf16[3,2,32,2,1024]{4,3,2,1,0:T(2,128)(2,1)}, u32[]{:S(2)}) copy-start(bf16[3,2,32,2,1024]{4,3,2,1,0:T(2,128)(2,1)} %copy-done.3) | copy-start | bytes 2359300
  29.1 11.5 %copy-start.2 = (bf16[512,512]{1,0:T(8,128)(2,1)S(1)}, bf16[512,512]{1,0:T(8,128)(2,1)}, u32[]{:S(2)}) copy-start(bf16[512,512]{1,0:T(8,128)(2,1)} %constant.10.clone.perm_ref) | copy-start | bytes 1572868
  31.6 23.2 %all-to-all-start = ((bf16[32,32,384]{2,1,0:T(8,128)(2,1)}), bf16[32,32,384]{2,1,0:T(8,128)(2,1)S(1)}, u32[]{:S(2)}, u32[]{:S(2)}) async-start(bf16[32,32,384]{2,1,0:T(8,128)(2,1)} %bitcast.14), calls=%async_computation | async-start | bytes 1572864 | tf_op jit(solution)/shard_map/all_to_all | solution.py:403
  54.8 23.3 %copy-start.1 = (bf16[1024,1024]{1,0:T(8,128)(2,1)S(1)}, bf16[1024,1024]{1,0:T(8,128)(2,1)}, u32[]{:S(2)}) copy-start(bf16[1024,1024]{1,0:T(8,128)(2,1)} %constant.11.clone.table_ref) | copy-start | bytes 6291460

commit v3 on v2

--- a/solution.py
+++ b/solution.py
@@ -63,30 +63,29 @@
     )
 
 
-def stage_kernel(x_ref, out_ref, sem):
-    fields, parts, slots = out_ref.shape[:3]
+def stage_kernel(x_ref, out_ref, held, sem):
+    fields, parts, slots = held.shape[:3]
     copies = []
     for field in range(fields):
         for part in range(parts):
             for half in range(2):
                 area = (field, part, pl.ds(half * (slots // 2), slots // 2))
                 copies.append(pltpu.make_async_copy(
-                    x_ref.at[area], out_ref.at[area], sem.at[len(copies)]))
+                    x_ref.at[area], held.at[area], sem.at[len(copies)]))
                 copies[-1].start()
-    for copy in copies:
-        copy.wait()
+    rows = out_ref.shape[0] // fields
+    for field in range(fields):
+        for copy in copies[4 * field:4 * field + 4]:
+            copy.wait()
+        out_ref[field * rows:(field + 1) * rows, :] = held[field].reshape(rows, held.shape[-1])
 
 
 def stage(x):
-    return call(
-        stage_kernel, "stage", pltpu.VMEM((3,) + x.shape[1:], BF16),
-        [FAR], HERE, [pltpu.SemaphoreType.DMA((12,))],
+    rows, modes = 3 * math.prod(x.shape[1:-1]), x.shape[-1]
+    return call(
+        stage_kernel, "stage", pltpu.VMEM((rows, modes), BF16),
+        [FAR], HERE, [pltpu.VMEM((3,) + x.shape[1:], BF16), pltpu.SemaphoreType.DMA((12,))],
     )(in_hbm(x))
-
-
-def field_rows(ref, field):
-    block = ref[field]
-    return block.reshape(math.prod(block.shape[:-1]), block.shape[-1])
 
 
 def masked_rows(block, lens, weight):
@@ -176,18 +175,17 @@
 def slope_kernel(x_ref, low_ref, high_ref, lens_ref, weight_ref, rows_ref, table_ref, out_ref,
                  buffer, sem):
     held = []
+    count = x_ref.shape[0] // 3
     for field in range(3):
-        stacked = jnp.concatenate(
-            [field_rows(x_ref, field), field_rows(low_ref, field), field_rows(high_ref, field)],
-            axis=0,
-        )
+        rows = pl.ds(field * count, count)
+        stacked = jnp.concatenate([x_ref[rows, :], low_ref[rows, :], high_ref[rows, :]], axis=0)
         slope = dot(rows_ref[...], stacked, ((1,), (0,)))
         held.append(masked_rows(slope, lens_ref[...], weight_ref[...]))
     send_bands(table_ref, jnp.concatenate(held, axis=0), out_ref, buffer, sem)
 
 
 def radial_slope(x, low, high, lens, weight, rows_map, table):
-    rows = math.prod(x.shape[:-1])
+    rows = x.shape[0]
     return call(
         slope_kernel, "radial_slope", pltpu.HBM((R, rows), BF16), [HERE] * 7, FAR,
         [pltpu.VMEM((R, rows), BF16), pltpu.SemaphoreType.DMA((4,))],
@@ -420,9 +418,8 @@
     )
     raw_bands = exchange(bands)
     table = azimuthal_table(orders, slots)
-    later_lens, table = lax.optimization_barrier((lens, table))
     slope_bands = exchange(
-        radial_slope(sloped, low, high, later_lens, weight, rows_map, synthesis)
+        radial_slope(sloped, low, high, lens, weight, rows_map, synthesis)
     )
     axial = axial_stage(raw_bands, perm, table, groups, band)
     spectral = physical_stage(slope_bands, axial, perm, table, groups, band)

time: 80.3 us -> 79.7 us (level)
  local copies, waits for them, and re-layouts: 2.04 us -> 0.03 us
  Pallas kernels: 21.2 us -> 22.5 us
    ppermute x2, waiting for transfers between devices: 3.72 us -> 7.37 us  [shift(): lax.ppermute(block, 'axial', [(i, (i + offset) % count) for i in range(co...]
    all_to_all x2, waiting for transfers between devices: 11.5 us -> 7.91 us  [exchange(): lax.all_to_all(block, 'order', split_axis=0, concat_axis=0, tiled=True)]
    unnamed x14 -> x10, local copies, waits for them, and re-layouts: 2.04 us -> 0.03 us
    pallas_call x1, Pallas kernels: 2.47 us -> 3.77 us  [radial_slope(): call(slope_kernel, 'radial_slope', pltpu.HBM((R, rows), BF16), [HERE] * 7...]
  transfers between devices with their start and end apart: 4 -> 4, of which waited for: 3 -> 3; matrix products, arithmetic and copies ran while one was open for 0% -> 0% of each run, Pallas kernels for 16% -> 18%
where the time goes in v3:
time: 79.7 us; the launch traced here: 79.3 us
  starting transfers between devices  23.5 us (29%)
  Pallas kernels  22.5 us (28%)
  blocking collectives  17.9 us (22%)
  waiting for transfers between devices  15.3 us (19%)
    all_to_all x1, blocking collectives, exchange(): lax.all_to_all(block, 'order', split_axis=0, concat_axis=0, tiled=True)  17.9 us
    all_to_all x2, starting transfers between devices, exchange(): lax.all_to_all(block, 'order', split_axis=0, concat_axis=0, tiled=True)  17 us
    all_to_all x2, waiting for transfers between devices, exchange(): lax.all_to_all(block, 'order', split_axis=0, concat_axis=0, tiled=True)  7.91 us
    ppermute x2, waiting for transfers between devices, shift(): lax.ppermute(block, 'axial', [(i, (i + offset) % count) for i in range(co...  7.37 us
    ppermute x2, starting transfers between devices, shift(): lax.ppermute(block, 'axial', [(i, (i + offset) % count) for i in range(co...  6.48 us
    pallas_call x1, Pallas kernels, physical_stage(): call(functools.partial(physical_kernel, groups, band, step, scale), 'phys...  5.38 us
    pallas_call x1, Pallas kernels, radial_raw(): call(raw_kernel, 'radial_raw', (pltpu.HBM((R, rows), BF16), jax.ShapeDtyp...  3.97 us
    pallas_call x1, Pallas kernels, radial_slope(): call(slope_kernel, 'radial_slope', pltpu.HBM((R, rows), BF16), [HERE] * 7...  3.77 us
  transfers between devices with their start and end apart: 4, of which 3 were waited for; matrix products, arithmetic and copies ran while one was open for 0% of the time, Pallas kernels for 18%

profile of v3, /device:TPU:1, one launch (start us, length us, event | category | flops | bytes accessed | tf_op | source)
XLA Modules:
  0.0 79.3 jit_solution(18213700573865320814)
XLA Ops:
  0.0 1.3 %stage.1.x_ref = bf16[384,1024]{1,0:T(8,128)(2,1)S(1)} custom-call(bf16[4,2,32,2,1024]{4,3,2,1,0:T(2,128)(2,1)} %x_far.1), custom_call_target="tpu_custom_call" | custom-call | tf_op jit(solution)/shard_map/stage/pallas_call | solution.py:85
  1.3 0.0 copy-start
  1.3 0.0 copy-start.3
  1.3 6.5 %collective-permute-start.1 = (bf16[384,1024]{1,0:T(8,128)(2,1)S(1)}, bf16[384,1024]{1,0:T(8,128)(2,1)}, u32[]{:S(2)}, u32[]{:S(2)}) collective-permute-start(bf16[384,1024]{1,0:T(8,128)(2,1)S(1)} %stage.1.x_ref), channel_id=1, source_target_pairs={{0,7},{1,0},{2,1},{3,2},{4,3},{5,4},{6,5},{7,6},{8,15},{9,8},{10,9... | collective-permute-start | bytes 2359304 | tf_op jit(solution)/shard_map/ppermute | solution.py:397
  7.8 0.0 collective-permute-start
  7.8 4.0 %radial_raw.1 = (bf16[1024,128]{1,0:T(8,128)(2,1)}, s32[128,128]{1,0:T(8,128)S(1)}, f32[128,128]{1,0:T(8,128)S(1)}) custom-call(s32[8,128]{1,0:T(8,128)} %bitcast.12, s32[8,128]{1,0:T(8,128)} %bitcast.16, bf16[4,2,32,2,1024]{4,3,2,1,0:T(2,128)(2,1)} %x_far.1, bf16[1024,1024]{1,0:T(8,128)(2,1)} %constant.8.clone.table_far.table_ref), custom_call_target="tpu_custom_call" | custom-call | tf_op jit(solution)/shard_map/radial_raw/pallas_call | solution.py:162
  11.8 8.1 %all-to-all-start.1 = ((bf16[32,32,128]{2,1,0:T(8,128)(2,1)}), bf16[32,32,128]{2,1,0:T(8,128)(2,1)S(1)}, u32[]{:S(2)}, u32[]{:S(2)}) async-start(bf16[32,32,128]{2,1,0:T(8,128)(2,1)} %bitcast.15), calls=%async_computation.1 | async-start | bytes 524288 | tf_op jit(solution)/shard_map/all_to_all | solution.py:401
  19.8 4.2 %collective-permute-done.1.high_ref = bf16[384,1024]{1,0:T(8,128)(2,1)} collective-permute-done((bf16[384,1024]{1,0:T(8,128)(2,1)S(1)}, bf16[384,1024]{1,0:T(8,128)(2,1)}, u32[]{:S(2)}, u32[]{:S(2)}) %collective-permute-start.1) | collective-permute-done | bytes 786464 | tf_op jit(solution)/shard_map/ppermute | solution.py:397
  24.0 3.2 %collective-permute-done.low_ref = bf16[384,1024]{1,0:T(8,128)(2,1)} collective-permute-done((bf16[384,1024]{1,0:T(8,128)(2,1)S(1)}, bf16[384,1024]{1,0:T(8,128)(2,1)}, u32[]{:S(2)}, u32[]{:S(2)}) %collective-permute-start) | collective-permute-done | bytes 786464 | tf_op jit(solution)/shard_map/ppermute | solution.py:397
  27.2 0.0 copy-done
  27.2 0.0 copy-done.3
  27.2 0.0 copy-start.4
  27.2 3.8 %radial_slope.1 = bf16[1024,384]{1,0:T(8,128)(2,1)} custom-call(bf16[384,1024]{1,0:T(8,128)(2,1)S(1)} %stage.1.x_ref, bf16[384,1024]{1,0:T(8,128)(2,1)} %collective-permute-done.low_ref, bf16[384,1024]{1,0:T(8,128)(2,1)} %collective-permute-done.1.high_ref, s32[128,128]{1,0:T(8,128)S(1)} %get-tuple-element.8.lens_ref, ...), custom_call_target="tpu_custom_call" | custom-call | tf_op jit(solution)/shard_map/radial_slope/pallas_call | solution.py:189
  31.0 0.0 all-to-all-done.1
  31.0 9.0 %all-to-all-start = ((bf16[32,32,384]{2,1,0:T(8,128)(2,1)}), bf16[32,32,384]{2,1,0:T(8,128)(2,1)S(1)}, u32[]{:S(2)}, u32[]{:S(2)}) async-start(bf16[32,32,384]{2,1,0:T(8,128)(2,1)} %bitcast.14), calls=%async_computation | async-start | bytes 1572864 | tf_op jit(solution)/shard_map/all_to_all | solution.py:401
  40.0 0.0 copy-done.4
  40.0 0.0 copy-start.2
  40.0 3.5 %azimuthal_table.1.far_ref = bf16[1024,2176]{1,0:T(8,128)(2,1)} custom-call(s32[8,128]{1,0:T(8,128)S(1)} %bitcast.13), custom_call_target="tpu_custom_call" | custom-call | tf_op jit(solution)/shard_map/azimuthal_table/pallas_call | solution.py:239
  43.5 0.0 copy-done.2
  43.5 2.8 %axial_stage.1.axial_ref = f32[64,2176]{1,0:T(8,128)S(1)} custom-call(bf16[1024,128]{1,0:T(8,128)(2,1)S(1)} %bitcast.11, bf16[512,512]{1,0:T(8,128)(2,1)S(1)} %copy-done.2, bf16[1024,2176]{1,0:T(8,128)(2,1)} %azimuthal_table.1.far_ref), custom_call_target="tpu_custom_call" | custom-call | tf_op jit(solution)/shard_map/axial_stage/pallas_call | solution.py:297
  46.3 7.9 %all-to-all-done = bf16[32,32,384]{2,1,0:T(8,128)(2,1)S(1)} async-done(((bf16[32,32,384]{2,1,0:T(8,128)(2,1)}), bf16[32,32,384]{2,1,0:T(8,128)(2,1)S(1)}, u32[]{:S(2)}, u32[]{:S(2)}) %all-to-all-start) | async-done | bytes 786464 | tf_op jit(solution)/shard_map/all_to_all | solution.py:401
  54.2 0.0 copy-start.1
  54.2 5.4 %physical_stage.1 = bf16[1024,384]{1,0:T(8,128)(2,1)S(1)} custom-call(bf16[1024,384]{1,0:T(8,128)(2,1)S(1)} %bitcast.8, f32[64,2176]{1,0:T(8,128)S(1)} %axial_stage.1.axial_ref, bf16[512,512]{1,0:T(8,128)(2,1)S(1)} %copy-done.2, bf16[1024,2176]{1,0:T(8,128)(2,1)} %azimuthal_table.1.far_ref), custom_call_target="tpu_custom_call" | custom-call | tf_op jit(solution)/shard_map/physical_stage/pallas_call | solution.py:362
  59.6 17.9 %all_to_all.33 = bf16[32,32,384]{2,1,0:T(8,128)(2,1)S(1)} all-to-all(bf16[32,32,384]{2,1,0:T(8,128)(2,1)S(1)} %bitcast.9), channel_id=1, replica_groups=mesh['order'=32,'axial'=8] {'order'}, dimensions={0} | all-to-all | bytes 1572864 | tf_op jit(solution)/shard_map/all_to_all | solution.py:401
  77.4 0.0 copy-done.1
  77.5 1.8 %radial_analysis.1 = bf16[3,2,32,2,1024]{4,3,2,1,0:T(2,128)(2,1)} custom-call(bf16[1024,384]{1,0:T(8,128)(2,1)S(1)} %bitcast.10, s32[128,128]{1,0:T(8,128)S(1)} %get-tuple-element.8.lens_ref, bf16[1024,1024]{1,0:T(8,128)(2,1)S(1)} %copy-done.1), custom_call_target="tpu_custom_call" | custom-call | tf_op jit(solution)/shard_map/radial_analysis/pallas_call | solution.py:389
Async XLA Ops:
  1.3 25.9 %copy-start = (bf16[1024,1024]{1,0:T(8,128)(2,1)S(1)}, bf16[1024,1024]{1,0:T(8,128)(2,1)}, u32[]{:S(2)}) copy-start(bf16[1024,1024]{1,0:T(8,128)(2,1)} %constant.8.clone.table_far.table_ref) | copy-start | bytes 6291460
  1.3 25.9 %copy-start.3 = (bf16[128,384]{1,0:T(8,128)(2,1)S(1)}, bf16[128,384]{1,0:T(8,128)(2,1)}, u32[]{:S(2)}) copy-start(bf16[128,384]{1,0:T(8,128)(2,1)} %constant.9.clone.rows_ref) | copy-start | bytes 294916
  1.3 22.7 %collective-permute-start.1 = (bf16[384,1024]{1,0:T(8,128)(2,1)S(1)}, bf16[384,1024]{1,0:T(8,128)(2,1)}, u32[]{:S(2)}, u32[]{:S(2)}) collective-permute-start(bf16[384,1024]{1,0:T(8,128)(2,1)S(1)} %stage.1.x_ref), channel_id=1, source_target_pairs={{0,7},{1,0},{2,1},{3,2},{4,3},{5,4},{6,5},{7,6},{8,15},{9,8},{10,9... | collective-permute-start | bytes 2359304 | tf_op jit(solution)/shard_map/ppermute | solution.py:397
  7.8 19.4 %collective-permute-start = (bf16[384,1024]{1,0:T(8,128)(2,1)S(1)}, bf16[384,1024]{1,0:T(8,128)(2,1)}, u32[]{:S(2)}, u32[]{:S(2)}) collective-permute-start(bf16[384,1024]{1,0:T(8,128)(2,1)S(1)} %stage.1.x_ref), channel_id=1, source_target_pairs={{0,1},{1,2},{2,3},{3,4},{4,5},{5,6},{6,7},{7,0},{8,9},{9,10},{10,1... | collective-permute-start | bytes 2359304 | tf_op jit(solution)/shard_map/ppermute | solution.py:397
  11.8 19.2 %all-to-all-start.1 = ((bf16[32,32,128]{2,1,0:T(8,128)(2,1)}), bf16[32,32,128]{2,1,0:T(8,128)(2,1)S(1)}, u32[]{:S(2)}, u32[]{:S(2)}) async-start(bf16[32,32,128]{2,1,0:T(8,128)(2,1)} %bitcast.15), calls=%async_computation.1 | async-start | bytes 524288 | tf_op jit(solution)/shard_map/all_to_all | solution.py:401
  27.2 12.8 %copy-start.4 = (s32[1024]{0:T(1024)S(1)}, s32[1024]{0:T(1024)}, u32[]{:S(2)}) copy-start(s32[1024]{0:T(1024)} %param.8) | copy-start | bytes 12292
  31.0 23.2 %all-to-all-start = ((bf16[32,32,384]{2,1,0:T(8,128)(2,1)}), bf16[32,32,384]{2,1,0:T(8,128)(2,1)S(1)}, u32[]{:S(2)}, u32[]{:S(2)}) async-start(bf16[32,32,384]{2,1,0:T(8,128)(2,1)} %bitcast.14), calls=%async_computation | async-start | bytes 1572864 | tf_op jit(solution)/shard_map/all_to_all | solution.py:401
  40.0 3.5 %copy-start.2 = (bf16[512,512]{1,0:T(8,128)(2,1)S(1)}, bf16[512,512]{1,0:T(8,128)(2,1)}, u32[]{:S(2)}) copy-start(bf16[512,512]{1,0:T(8,128)(2,1)} %constant.10.clone.perm_ref) | copy-start | bytes 1572868
  54.2 23.3 %copy-start.1 = (bf16[1024,1024]{1,0:T(8,128)(2,1)S(1)}, bf16[1024,1024]{1,0:T(8,128)(2,1)}, u32[]{:S(2)}) copy-start(bf16[1024,1024]{1,0:T(8,128)(2,1)} %constant.11.clone.table_ref) | copy-start | bytes 6291460

commit v4 on v3

--- a/solution.py
+++ b/solution.py
@@ -172,8 +172,19 @@
     )(in_hbm(orders), in_hbm(lengths), in_hbm(x), in_hbm(table))
 
 
-def slope_kernel(x_ref, low_ref, high_ref, lens_ref, weight_ref, rows_ref, table_ref, out_ref,
-                 buffer, sem):
+def row_loads(far_ref, held, sem, count=4):
+    size = held.shape[0] // count
+    loads = []
+    for i in range(count):
+        rows = pl.ds(i * size, size)
+        loads.append(pltpu.make_async_copy(far_ref.at[rows], held.at[rows], sem.at[i]))
+        loads[-1].start()
+    return loads
+
+
+def slope_kernel(x_ref, low_ref, high_ref, lens_ref, weight_ref, rows_ref, table_far, out_ref,
+                 buffer, sem, table, load_sem):
+    loads = row_loads(table_far, table, load_sem)
     held = []
     count = x_ref.shape[0] // 3
     for field in range(3):
@@ -181,15 +192,16 @@
         stacked = jnp.concatenate([x_ref[rows, :], low_ref[rows, :], high_ref[rows, :]], axis=0)
         slope = dot(rows_ref[...], stacked, ((1,), (0,)))
         held.append(masked_rows(slope, lens_ref[...], weight_ref[...]))
-    send_bands(table_ref, jnp.concatenate(held, axis=0), out_ref, buffer, sem)
+    send_bands(table, jnp.concatenate(held, axis=0), out_ref, buffer, sem, loads)
 
 
 def radial_slope(x, low, high, lens, weight, rows_map, table):
     rows = x.shape[0]
     return call(
-        slope_kernel, "radial_slope", pltpu.HBM((R, rows), BF16), [HERE] * 7, FAR,
-        [pltpu.VMEM((R, rows), BF16), pltpu.SemaphoreType.DMA((4,))],
-    )(x, low, high, lens, weight, rows_map, table)
+        slope_kernel, "radial_slope", pltpu.HBM((R, rows), BF16), [HERE] * 6 + [FAR], FAR,
+        [pltpu.VMEM((R, rows), BF16), pltpu.SemaphoreType.DMA((4,)),
+         pltpu.VMEM(table.shape, BF16), pltpu.SemaphoreType.DMA((4,))],
+    )(x, low, high, lens, weight, rows_map, in_hbm(table))
 
 
 def sine_cosine(phase, points):

time: 79.7 us -> 80 us (level)
  no operation moved by 1% of the time
where the time goes in v4:
time: 80 us; the launch traced here: 79.5 us
  starting transfers between devices  23.5 us (29%)
  Pallas kernels  22.9 us (29%)
  blocking collectives  17.9 us (22%)
  waiting for transfers between devices  15.2 us (19%)
    all_to_all x1, blocking collectives, exchange(): lax.all_to_all(block, 'order', split_axis=0, concat_axis=0, tiled=True)  17.9 us
    all_to_all x2, starting transfers between devices, exchange(): lax.all_to_all(block, 'order', split_axis=0, concat_axis=0, tiled=True)  17 us
    all_to_all x2, waiting for transfers between devices, exchange(): lax.all_to_all(block, 'order', split_axis=0, concat_axis=0, tiled=True)  7.92 us
    ppermute x2, waiting for transfers between devices, shift(): lax.ppermute(block, 'axial', [(i, (i + offset) % count) for i in range(co...  7.26 us
    ppermute x2, starting transfers between devices, shift(): lax.ppermute(block, 'axial', [(i, (i + offset) % count) for i in range(co...  6.48 us
    pallas_call x1, Pallas kernels, physical_stage(): call(functools.partial(physical_kernel, groups, band, step, scale), 'phys...  5.38 us
    pallas_call x1, Pallas kernels, radial_slope(): call(slope_kernel, 'radial_slope', pltpu.HBM((R, rows), BF16), [HERE] * 6...  4.11 us
    pallas_call x1, Pallas kernels, radial_raw(): call(raw_kernel, 'radial_raw', (pltpu.HBM((R, rows), BF16), jax.ShapeDtyp...  3.97 us
  transfers between devices with their start and end apart: 4, of which 3 were waited for; matrix products, arithmetic and copies ran while one was open for 0% of the time, Pallas kernels for 18%

profile of v4, /device:TPU:1, one launch (start us, length us, event | category | flops | bytes accessed | tf_op | source)
XLA Modules:
  0.0 79.5 jit_solution(6898037461818629756)
XLA Ops:
  0.0 1.3 %stage.1.x_ref = bf16[384,1024]{1,0:T(8,128)(2,1)S(1)} custom-call(bf16[4,2,32,2,1024]{4,3,2,1,0:T(2,128)(2,1)} %x_far.1), custom_call_target="tpu_custom_call" | custom-call | tf_op jit(solution)/shard_map/stage/pallas_call | solution.py:85
  1.3 0.0 copy-start.2
  1.3 6.5 %collective-permute-start.1 = (bf16[384,1024]{1,0:T(8,128)(2,1)S(1)}, bf16[384,1024]{1,0:T(8,128)(2,1)S(1)}, u32[]{:S(2)}, u32[]{:S(2)}) collective-permute-start(bf16[384,1024]{1,0:T(8,128)(2,1)S(1)} %stage.1.x_ref), channel_id=1, source_target_pairs={{0,7},{1,0},{2,1},{3,2},{4,3},{5,4},{6,5},{7,6},{8,15},{9,8},{10,9... | collective-permute-start | bytes 2359304 | tf_op jit(solution)/shard_map/ppermute | solution.py:409
  7.8 0.0 collective-permute-start
  7.8 4.0 %radial_raw.1 = (bf16[1024,128]{1,0:T(8,128)(2,1)}, s32[128,128]{1,0:T(8,128)S(1)}, f32[128,128]{1,0:T(8,128)S(1)}) custom-call(s32[8,128]{1,0:T(8,128)} %bitcast.12, s32[8,128]{1,0:T(8,128)} %bitcast.16, bf16[4,2,32,2,1024]{4,3,2,1,0:T(2,128)(2,1)} %x_far.1, bf16[1024,1024]{1,0:T(8,128)(2,1)} %constant.8.clone.table_far), custom_call_target="tpu_custom_call" | custom-call | tf_op jit(solution)/shard_map/radial_raw/pallas_call | solution.py:162
  11.8 8.1 %all-to-all-start.1 = ((bf16[32,32,128]{2,1,0:T(8,128)(2,1)}), bf16[32,32,128]{2,1,0:T(8,128)(2,1)S(1)}, u32[]{:S(2)}, u32[]{:S(2)}) async-start(bf16[32,32,128]{2,1,0:T(8,128)(2,1)} %bitcast.15), calls=%async_computation.1 | async-start | bytes 524288 | tf_op jit(solution)/shard_map/all_to_all | solution.py:413
  19.8 4.2 %collective-permute-done.1.high_ref = bf16[384,1024]{1,0:T(8,128)(2,1)S(1)} collective-permute-done((bf16[384,1024]{1,0:T(8,128)(2,1)S(1)}, bf16[384,1024]{1,0:T(8,128)(2,1)S(1)}, u32[]{:S(2)}, u32[]{:S(2)}) %collective-permute-start.1) | collective-permute-done | bytes 786464 | tf_op jit(solution)/shard_map/ppermute | solution.py:409
  24.0 3.1 %collective-permute-done.low_ref = bf16[384,1024]{1,0:T(8,128)(2,1)S(1)} collective-permute-done((bf16[384,1024]{1,0:T(8,128)(2,1)S(1)}, bf16[384,1024]{1,0:T(8,128)(2,1)S(1)}, u32[]{:S(2)}, u32[]{:S(2)}) %collective-permute-start) | collective-permute-done | bytes 786464 | tf_op jit(solution)/shard_map/ppermute | solution.py:409
  27.1 0.0 copy-done.2
  27.1 0.0 copy-start.3
  27.1 4.1 %radial_slope.1 = bf16[1024,384]{1,0:T(8,128)(2,1)} custom-call(bf16[384,1024]{1,0:T(8,128)(2,1)S(1)} %stage.1.x_ref, bf16[384,1024]{1,0:T(8,128)(2,1)S(1)} %collective-permute-done.low_ref, bf16[384,1024]{1,0:T(8,128)(2,1)S(1)} %collective-permute-done.1.high_ref, s32[128,128]{1,0:T(8,128)S(1)} %get-tuple-element.8.lens_ref, ...), custom_call_target="tpu_custom_call" | custom-call | tf_op jit(solution)/shard_map/radial_slope/pallas_call | solution.py:200
  31.2 0.0 all-to-all-done.1
  31.2 9.0 %all-to-all-start = ((bf16[32,32,384]{2,1,0:T(8,128)(2,1)}), bf16[32,32,384]{2,1,0:T(8,128)(2,1)S(1)}, u32[]{:S(2)}, u32[]{:S(2)}) async-start(bf16[32,32,384]{2,1,0:T(8,128)(2,1)} %bitcast.14), calls=%async_computation | async-start | bytes 1572864 | tf_op jit(solution)/shard_map/all_to_all | solution.py:413
  40.2 0.0 copy-done.3
  40.2 0.0 copy-start.1
  40.2 3.5 %azimuthal_table.1.far_ref = bf16[1024,2176]{1,0:T(8,128)(2,1)} custom-call(s32[8,128]{1,0:T(8,128)S(1)} %bitcast.13), custom_call_target="tpu_custom_call" | custom-call | tf_op jit(solution)/shard_map/azimuthal_table/pallas_call | solution.py:251
  43.7 0.0 copy-done.1
  43.8 2.8 %axial_stage.1.axial_ref = f32[64,2176]{1,0:T(8,128)S(1)} custom-call(bf16[1024,128]{1,0:T(8,128)(2,1)S(1)} %bitcast.11, bf16[512,512]{1,0:T(8,128)(2,1)S(1)} %copy-done.1, bf16[1024,2176]{1,0:T(8,128)(2,1)} %azimuthal_table.1.far_ref), custom_call_target="tpu_custom_call" | custom-call | tf_op jit(solution)/shard_map/axial_stage/pallas_call | solution.py:309
  46.5 7.9 %all-to-all-done = bf16[32,32,384]{2,1,0:T(8,128)(2,1)S(1)} async-done(((bf16[32,32,384]{2,1,0:T(8,128)(2,1)}), bf16[32,32,384]{2,1,0:T(8,128)(2,1)S(1)}, u32[]{:S(2)}, u32[]{:S(2)}) %all-to-all-start) | async-done | bytes 786464 | tf_op jit(solution)/shard_map/all_to_all | solution.py:413
  54.4 0.0 copy-start
  54.4 5.4 %physical_stage.1 = bf16[1024,384]{1,0:T(8,128)(2,1)S(1)} custom-call(bf16[1024,384]{1,0:T(8,128)(2,1)S(1)} %bitcast.8, f32[64,2176]{1,0:T(8,128)S(1)} %axial_stage.1.axial_ref, bf16[512,512]{1,0:T(8,128)(2,1)S(1)} %copy-done.1, bf16[1024,2176]{1,0:T(8,128)(2,1)} %azimuthal_table.1.far_ref), custom_call_target="tpu_custom_call" | custom-call | tf_op jit(solution)/shard_map/physical_stage/pallas_call | solution.py:374
  59.8 17.9 %all_to_all.33 = bf16[32,32,384]{2,1,0:T(8,128)(2,1)S(1)} all-to-all(bf16[32,32,384]{2,1,0:T(8,128)(2,1)S(1)} %bitcast.9), channel_id=1, replica_groups=mesh['order'=32,'axial'=8] {'order'}, dimensions={0} | all-to-all | bytes 1572864 | tf_op jit(solution)/shard_map/all_to_all | solution.py:413
  77.7 0.0 copy-done
  77.7 1.8 %radial_analysis.1 = bf16[3,2,32,2,1024]{4,3,2,1,0:T(2,128)(2,1)} custom-call(bf16[1024,384]{1,0:T(8,128)(2,1)S(1)} %bitcast.10, s32[128,128]{1,0:T(8,128)S(1)} %get-tuple-element.8.lens_ref, bf16[1024,1024]{1,0:T(8,128)(2,1)S(1)} %copy-done), custom_call_target="tpu_custom_call" | custom-call | tf_op jit(solution)/shard_map/radial_analysis/pallas_call | solution.py:401
Async XLA Ops:
  1.3 25.8 %copy-start.2 = (bf16[128,384]{1,0:T(8,128)(2,1)S(1)}, bf16[128,384]{1,0:T(8,128)(2,1)}, u32[]{:S(2)}) copy-start(bf16[128,384]{1,0:T(8,128)(2,1)} %constant.9.clone.rows_ref) | copy-start | bytes 294916
  1.3 22.7 %collective-permute-start.1 = (bf16[384,1024]{1,0:T(8,128)(2,1)S(1)}, bf16[384,1024]{1,0:T(8,128)(2,1)S(1)}, u32[]{:S(2)}, u32[]{:S(2)}) collective-permute-start(bf16[384,1024]{1,0:T(8,128)(2,1)S(1)} %stage.1.x_ref), channel_id=1, source_target_pairs={{0,7},{1,0},{2,1},{3,2},{4,3},{5,4},{6,5},{7,6},{8,15},{9,8},{10,9... | collective-permute-start | bytes 2359304 | tf_op jit(solution)/shard_map/ppermute | solution.py:409
  7.8 19.3 %collective-permute-start = (bf16[384,1024]{1,0:T(8,128)(2,1)S(1)}, bf16[384,1024]{1,0:T(8,128)(2,1)S(1)}, u32[]{:S(2)}, u32[]{:S(2)}) collective-permute-start(bf16[384,1024]{1,0:T(8,128)(2,1)S(1)} %stage.1.x_ref), channel_id=1, source_target_pairs={{0,1},{1,2},{2,3},{3,4},{4,5},{5,6},{6,7},{7,0},{8,9},{9,10},{10,1... | collective-permute-start | bytes 2359304 | tf_op jit(solution)/shard_map/ppermute | solution.py:409
  11.8 19.4 %all-to-all-start.1 = ((bf16[32,32,128]{2,1,0:T(8,128)(2,1)}), bf16[32,32,128]{2,1,0:T(8,128)(2,1)S(1)}, u32[]{:S(2)}, u32[]{:S(2)}) async-start(bf16[32,32,128]{2,1,0:T(8,128)(2,1)} %bitcast.15), calls=%async_computation.1 | async-start | bytes 524288 | tf_op jit(solution)/shard_map/all_to_all | solution.py:413
  27.1 13.1 %copy-start.3 = (s32[1024]{0:T(1024)S(1)}, s32[1024]{0:T(1024)}, u32[]{:S(2)}) copy-start(s32[1024]{0:T(1024)} %param.8) | copy-start | bytes 12292
  31.2 23.2 %all-to-all-start = ((bf16[32,32,384]{2,1,0:T(8,128)(2,1)}), bf16[32,32,384]{2,1,0:T(8,128)(2,1)S(1)}, u32[]{:S(2)}, u32[]{:S(2)}) async-start(bf16[32,32,384]{2,1,0:T(8,128)(2,1)} %bitcast.14), calls=%async_computation | async-start | bytes 1572864 | tf_op jit(solution)/shard_map/all_to_all | solution.py:413
  40.2 3.5 %copy-start.1 = (bf16[512,512]{1,0:T(8,128)(2,1)S(1)}, bf16[512,512]{1,0:T(8,128)(2,1)}, u32[]{:S(2)}) copy-start(bf16[512,512]{1,0:T(8,128)(2,1)} %constant.10.clone.perm_ref) | copy-start | bytes 1572868
  54.4 23.3 %copy-start = (bf16[1024,1024]{1,0:T(8,128)(2,1)S(1)}, bf16[1024,1024]{1,0:T(8,128)(2,1)}, u32[]{:S(2)}) copy-start(bf16[1024,1024]{1,0:T(8,128)(2,1)} %constant.11.clone.table_ref) | copy-start | bytes 6291460

commit v5 on v4

--- a/solution.py
+++ b/solution.py
@@ -93,13 +93,25 @@
     return jnp.where(modes < lens[:, :1], block.astype(F32) * weight[:, :1], 0.0).astype(BF16)
 
 
+def row_loads(far_ref, held, sem, count=16):
+    size = held.shape[0] // count
+    loads = []
+    for i in range(count):
+        rows = pl.ds(i * size, size)
+        loads.append(pltpu.make_async_copy(far_ref.at[rows], held.at[rows], sem.at[i]))
+        loads[-1].start()
+    return loads
+
+
 def send_bands(table_ref, rows, out_ref, buffer, sem, loads=None, count=4):
     size = table_ref.shape[0] // count
     copies = []
     for i in range(count):
         part = pl.ds(i * size, size)
         if loads is not None:
-            loads[i].wait()
+            share = len(loads) // count
+            for load in loads[i * share:(i + 1) * share]:
+                load.wait()
         buffer[part, :] = dot(table_ref[part, :], rows, ((1,), (1,))).astype(BF16)
         copies.append(pltpu.make_async_copy(buffer.at[part], out_ref.at[part], sem.at[i]))
         copies[-1].start()
@@ -131,20 +143,15 @@
 
 def raw_kernel(orders_far, lengths_far, x_far, table_far, out_ref, lens_ref, weight_ref,
                buffer, sem, orders, lengths, x_ref, small_sem, table, load_sem):
-    size = table.shape[0] // 4
     small = [
         pltpu.make_async_copy(orders_far, orders, small_sem.at[0]),
         pltpu.make_async_copy(lengths_far, lengths, small_sem.at[1]),
         pltpu.make_async_copy(x_far.at[3, 0], x_ref.at[0], small_sem.at[2]),
         pltpu.make_async_copy(x_far.at[3, 1], x_ref.at[1], small_sem.at[3]),
     ]
-    loads = [
-        pltpu.make_async_copy(table_far.at[pl.ds(i * size, size)],
-                              table.at[pl.ds(i * size, size)], load_sem.at[i])
-        for i in range(4)
-    ]
-    for copy in small + loads:
+    for copy in small:
         copy.start()
+    loads = row_loads(table_far, table, load_sem)
     small[0].wait()
     small[1].wait()
     lens, weight = slot_rows(orders, lengths, x_ref.shape[1])
@@ -168,18 +175,8 @@
         [pltpu.VMEM((R, rows), BF16), pltpu.SemaphoreType.DMA((4,)),
          pltpu.VMEM(orders.shape, jnp.int32), pltpu.VMEM(lengths.shape, jnp.int32),
          pltpu.VMEM(x.shape[1:], BF16), pltpu.SemaphoreType.DMA((4,)),
-         pltpu.VMEM(table.shape, BF16), pltpu.SemaphoreType.DMA((4,))],
+         pltpu.VMEM(table.shape, BF16), pltpu.SemaphoreType.DMA((16,))],
     )(in_hbm(orders), in_hbm(lengths), in_hbm(x), in_hbm(table))
-
-
-def row_loads(far_ref, held, sem, count=4):
-    size = held.shape[0] // count
-    loads = []
-    for i in range(count):
-        rows = pl.ds(i * size, size)
-        loads.append(pltpu.make_async_copy(far_ref.at[rows], held.at[rows], sem.at[i]))
-        loads[-1].start()
-    return loads
 
 
 def slope_kernel(x_ref, low_ref, high_ref, lens_ref, weight_ref, rows_ref, table_far, out_ref,
@@ -200,7 +197,7 @@
     return call(
         slope_kernel, "radial_slope", pltpu.HBM((R, rows), BF16), [HERE] * 6 + [FAR], FAR,
         [pltpu.VMEM((R, rows), BF16), pltpu.SemaphoreType.DMA((4,)),
-         pltpu.VMEM(table.shape, BF16), pltpu.SemaphoreType.DMA((4,))],
+         pltpu.VMEM(table.shape, BF16), pltpu.SemaphoreType.DMA((16,))],
     )(x, low, high, lens, weight, rows_map, in_hbm(table))
 
 

time: 80 us -> 80.1 us (level)
  transfers between devices with their start and end apart: 4 -> 4, of which waited for: 3 -> 3; matrix products, arithmetic and copies ran while one was open for 0% -> 0% of each run, Pallas kernels for 18% -> 19%
where the time goes in v5:
time: 80.1 us; the launch traced here: 79.7 us
  Pallas kernels  23.5 us (29%)
  starting transfers between devices  23.5 us (29%)
  blocking collectives  17.8 us (22%)
  waiting for transfers between devices  14.7 us (18%)
    all_to_all x1, blocking collectives, exchange(): lax.all_to_all(block, 'order', split_axis=0, concat_axis=0, tiled=True)  17.8 us
    all_to_all x2, starting transfers between devices, exchange(): lax.all_to_all(block, 'order', split_axis=0, concat_axis=0, tiled=True)  17 us
    all_to_all x2, waiting for transfers between devices, exchange(): lax.all_to_all(block, 'order', split_axis=0, concat_axis=0, tiled=True)  7.92 us
    ppermute x2, waiting for transfers between devices, shift(): lax.ppermute(block, 'axial', [(i, (i + offset) % count) for i in range(co...  6.81 us
    ppermute x2, starting transfers between devices, shift(): lax.ppermute(block, 'axial', [(i, (i + offset) % count) for i in range(co...  6.48 us
    pallas_call x1, Pallas kernels, physical_stage(): call(functools.partial(physical_kernel, groups, band, step, scale), 'phys...  5.39 us
    pallas_call x1, Pallas kernels, radial_raw(): call(raw_kernel, 'radial_raw', (pltpu.HBM((R, rows), BF16), jax.ShapeDtyp...  4.42 us
    pallas_call x1, Pallas kernels, radial_slope(): call(slope_kernel, 'radial_slope', pltpu.HBM((R, rows), BF16), [HERE] * 6...  4.29 us
  transfers between devices with their start and end apart: 4, of which 3 were waited for; matrix products, arithmetic and copies ran while one was open for 0% of the time, Pallas kernels for 19%

profile of v5, /device:TPU:1, one launch (start us, length us, event | category | flops | bytes accessed | tf_op | source)
XLA Modules:
  0.0 79.7 jit_solution(10223454130579396658)
XLA Ops:
  0.0 1.3 %stage.1.x_ref = bf16[384,1024]{1,0:T(8,128)(2,1)S(1)} custom-call(bf16[4,2,32,2,1024]{4,3,2,1,0:T(2,128)(2,1)} %x_far.1), custom_call_target="tpu_custom_call" | custom-call | tf_op jit(solution)/shard_map/stage/pallas_call | solution.py:85
  1.3 0.0 copy-start.2
  1.3 6.5 %collective-permute-start.1 = (bf16[384,1024]{1,0:T(8,128)(2,1)S(1)}, bf16[384,1024]{1,0:T(8,128)(2,1)S(1)}, u32[]{:S(2)}, u32[]{:S(2)}) collective-permute-start(bf16[384,1024]{1,0:T(8,128)(2,1)S(1)} %stage.1.x_ref), channel_id=1, source_target_pairs={{0,7},{1,0},{2,1},{3,2},{4,3},{5,4},{6,5},{7,6},{8,15},{9,8},{10,9... | collective-permute-start | bytes 2359304 | tf_op jit(solution)/shard_map/ppermute | solution.py:406
  7.8 0.0 collective-permute-start
  7.8 4.4 %radial_raw.1 = (bf16[1024,128]{1,0:T(8,128)(2,1)}, s32[128,128]{1,0:T(8,128)S(1)}, f32[128,128]{1,0:T(8,128)S(1)}) custom-call(s32[8,128]{1,0:T(8,128)} %bitcast.12, s32[8,128]{1,0:T(8,128)} %bitcast.16, bf16[4,2,32,2,1024]{4,3,2,1,0:T(2,128)(2,1)} %x_far.1, bf16[1024,1024]{1,0:T(8,128)(2,1)} %constant.8.clone.table_far), custom_call_target="tpu_custom_call" | custom-call | tf_op jit(solution)/shard_map/radial_raw/pallas_call | solution.py:169
  12.2 8.1 %all-to-all-start.1 = ((bf16[32,32,128]{2,1,0:T(8,128)(2,1)}), bf16[32,32,128]{2,1,0:T(8,128)(2,1)S(1)}, u32[]{:S(2)}, u32[]{:S(2)}) async-start(bf16[32,32,128]{2,1,0:T(8,128)(2,1)} %bitcast.15), calls=%async_computation.1 | async-start | bytes 524288 | tf_op jit(solution)/shard_map/all_to_all | solution.py:410
  20.3 3.7 %collective-permute-done.1.high_ref = bf16[384,1024]{1,0:T(8,128)(2,1)S(1)} collective-permute-done((bf16[384,1024]{1,0:T(8,128)(2,1)S(1)}, bf16[384,1024]{1,0:T(8,128)(2,1)S(1)}, u32[]{:S(2)}, u32[]{:S(2)}) %collective-permute-start.1) | collective-permute-done | bytes 786464 | tf_op jit(solution)/shard_map/ppermute | solution.py:406
  24.0 3.1 %collective-permute-done.low_ref = bf16[384,1024]{1,0:T(8,128)(2,1)S(1)} collective-permute-done((bf16[384,1024]{1,0:T(8,128)(2,1)S(1)}, bf16[384,1024]{1,0:T(8,128)(2,1)S(1)}, u32[]{:S(2)}, u32[]{:S(2)}) %collective-permute-start) | collective-permute-done | bytes 786464 | tf_op jit(solution)/shard_map/ppermute | solution.py:406
  27.1 0.0 copy-done.2
  27.1 0.0 copy-start.3
  27.1 4.3 %radial_slope.1 = bf16[1024,384]{1,0:T(8,128)(2,1)} custom-call(bf16[384,1024]{1,0:T(8,128)(2,1)S(1)} %stage.1.x_ref, bf16[384,1024]{1,0:T(8,128)(2,1)S(1)} %collective-permute-done.low_ref, bf16[384,1024]{1,0:T(8,128)(2,1)S(1)} %collective-permute-done.1.high_ref, s32[128,128]{1,0:T(8,128)S(1)} %get-tuple-element.8.lens_ref, ...), custom_call_target="tpu_custom_call" | custom-call | tf_op jit(solution)/shard_map/radial_slope/pallas_call | solution.py:197
  31.4 0.0 all-to-all-done.1
  31.4 9.0 %all-to-all-start = ((bf16[32,32,384]{2,1,0:T(8,128)(2,1)}), bf16[32,32,384]{2,1,0:T(8,128)(2,1)S(1)}, u32[]{:S(2)}, u32[]{:S(2)}) async-start(bf16[32,32,384]{2,1,0:T(8,128)(2,1)} %bitcast.14), calls=%async_computation | async-start | bytes 1572864 | tf_op jit(solution)/shard_map/all_to_all | solution.py:410
  40.4 0.0 copy-done.3
  40.4 0.0 copy-start.1
  40.4 3.5 %azimuthal_table.1.far_ref = bf16[1024,2176]{1,0:T(8,128)(2,1)} custom-call(s32[8,128]{1,0:T(8,128)S(1)} %bitcast.13), custom_call_target="tpu_custom_call" | custom-call | tf_op jit(solution)/shard_map/azimuthal_table/pallas_call | solution.py:248
  43.9 0.0 copy-done.1
  43.9 2.8 %axial_stage.1.axial_ref = f32[64,2176]{1,0:T(8,128)S(1)} custom-call(bf16[1024,128]{1,0:T(8,128)(2,1)S(1)} %bitcast.11, bf16[512,512]{1,0:T(8,128)(2,1)S(1)} %copy-done.1, bf16[1024,2176]{1,0:T(8,128)(2,1)} %azimuthal_table.1.far_ref), custom_call_target="tpu_custom_call" | custom-call | tf_op jit(solution)/shard_map/axial_stage/pallas_call | solution.py:306
  46.7 7.9 %all-to-all-done = bf16[32,32,384]{2,1,0:T(8,128)(2,1)S(1)} async-done(((bf16[32,32,384]{2,1,0:T(8,128)(2,1)}), bf16[32,32,384]{2,1,0:T(8,128)(2,1)S(1)}, u32[]{:S(2)}, u32[]{:S(2)}) %all-to-all-start) | async-done | bytes 786464 | tf_op jit(solution)/shard_map/all_to_all | solution.py:410
  54.6 0.0 copy-start
  54.6 5.4 %physical_stage.1 = bf16[1024,384]{1,0:T(8,128)(2,1)S(1)} custom-call(bf16[1024,384]{1,0:T(8,128)(2,1)S(1)} %bitcast.8, f32[64,2176]{1,0:T(8,128)S(1)} %axial_stage.1.axial_ref, bf16[512,512]{1,0:T(8,128)(2,1)S(1)} %copy-done.1, bf16[1024,2176]{1,0:T(8,128)(2,1)} %azimuthal_table.1.far_ref), custom_call_target="tpu_custom_call" | custom-call | tf_op jit(solution)/shard_map/physical_stage/pallas_call | solution.py:371
  60.0 17.8 %all_to_all.33 = bf16[32,32,384]{2,1,0:T(8,128)(2,1)S(1)} all-to-all(bf16[32,32,384]{2,1,0:T(8,128)(2,1)S(1)} %bitcast.9), channel_id=1, replica_groups=mesh['order'=32,'axial'=8] {'order'}, dimensions={0} | all-to-all | bytes 1572864 | tf_op jit(solution)/shard_map/all_to_all | solution.py:410
  77.9 0.0 copy-done
  77.9 1.8 %radial_analysis.1 = bf16[3,2,32,2,1024]{4,3,2,1,0:T(2,128)(2,1)} custom-call(bf16[1024,384]{1,0:T(8,128)(2,1)S(1)} %bitcast.10, s32[128,128]{1,0:T(8,128)S(1)} %get-tuple-element.8.lens_ref, bf16[1024,1024]{1,0:T(8,128)(2,1)S(1)} %copy-done), custom_call_target="tpu_custom_call" | custom-call | tf_op jit(solution)/shard_map/radial_analysis/pallas_call | solution.py:398
Async XLA Ops:
  1.3 25.8 %copy-start.2 = (bf16[128,384]{1,0:T(8,128)(2,1)S(1)}, bf16[128,384]{1,0:T(8,128)(2,1)}, u32[]{:S(2)}) copy-start(bf16[128,384]{1,0:T(8,128)(2,1)} %constant.9.clone.rows_ref) | copy-start | bytes 294916
  1.3 22.7 %collective-permute-start.1 = (bf16[384,1024]{1,0:T(8,128)(2,1)S(1)}, bf16[384,1024]{1,0:T(8,128)(2,1)S(1)}, u32[]{:S(2)}, u32[]{:S(2)}) collective-permute-start(bf16[384,1024]{1,0:T(8,128)(2,1)S(1)} %stage.1.x_ref), channel_id=1, source_target_pairs={{0,7},{1,0},{2,1},{3,2},{4,3},{5,4},{6,5},{7,6},{8,15},{9,8},{10,9... | collective-permute-start | bytes 2359304 | tf_op jit(solution)/shard_map/ppermute | solution.py:406
  7.8 19.3 %collective-permute-start = (bf16[384,1024]{1,0:T(8,128)(2,1)S(1)}, bf16[384,1024]{1,0:T(8,128)(2,1)S(1)}, u32[]{:S(2)}, u32[]{:S(2)}) collective-permute-start(bf16[384,1024]{1,0:T(8,128)(2,1)S(1)} %stage.1.x_ref), channel_id=1, source_target_pairs={{0,1},{1,2},{2,3},{3,4},{4,5},{5,6},{6,7},{7,0},{8,9},{9,10},{10,1... | collective-permute-start | bytes 2359304 | tf_op jit(solution)/shard_map/ppermute | solution.py:406
  12.2 19.2 %all-to-all-start.1 = ((bf16[32,32,128]{2,1,0:T(8,128)(2,1)}), bf16[32,32,128]{2,1,0:T(8,128)(2,1)S(1)}, u32[]{:S(2)}, u32[]{:S(2)}) async-start(bf16[32,32,128]{2,1,0:T(8,128)(2,1)} %bitcast.15), calls=%async_computation.1 | async-start | bytes 524288 | tf_op jit(solution)/shard_map/all_to_all | solution.py:410
  27.1 13.3 %copy-start.3 = (s32[1024]{0:T(1024)S(1)}, s32[1024]{0:T(1024)}, u32[]{:S(2)}) copy-start(s32[1024]{0:T(1024)} %param.8) | copy-start | bytes 12292
  31.4 23.2 %all-to-all-start = ((bf16[32,32,384]{2,1,0:T(8,128)(2,1)}), bf16[32,32,384]{2,1,0:T(8,128)(2,1)S(1)}, u32[]{:S(2)}, u32[]{:S(2)}) async-start(bf16[32,32,384]{2,1,0:T(8,128)(2,1)} %bitcast.14), calls=%async_computation | async-start | bytes 1572864 | tf_op jit(solution)/shard_map/all_to_all | solution.py:410
  40.4 3.5 %copy-start.1 = (bf16[512,512]{1,0:T(8,128)(2,1)S(1)}, bf16[512,512]{1,0:T(8,128)(2,1)}, u32[]{:S(2)}) copy-start(bf16[512,512]{1,0:T(8,128)(2,1)} %constant.10.clone.perm_ref) | copy-start | bytes 1572868
  54.6 23.2 %copy-start = (bf16[1024,1024]{1,0:T(8,128)(2,1)S(1)}, bf16[1024,1024]{1,0:T(8,128)(2,1)}, u32[]{:S(2)}) copy-start(bf16[1024,1024]{1,0:T(8,128)(2,1)} %constant.11.clone.table_ref) | copy-start | bytes 6291460

commit v6 on v3

--- a/solution.py
+++ b/solution.py
@@ -418,8 +418,9 @@
     )
     raw_bands = exchange(bands)
     table = azimuthal_table(orders, slots)
+    raw_bands, later_synthesis = lax.optimization_barrier((raw_bands, jnp.asarray(synthesis)))
     slope_bands = exchange(
-        radial_slope(sloped, low, high, lens, weight, rows_map, synthesis)
+        radial_slope(sloped, low, high, lens, weight, rows_map, later_synthesis)
     )
     axial = axial_stage(raw_bands, perm, table, groups, band)
     spectral = physical_stage(slope_bands, axial, perm, table, groups, band)

time: 79.7 us -> 78.2 us (0.981)
  blocking collectives: 17.9 us -> 34.9 us
  starting transfers between devices: 23.5 us -> 13.7 us
  waiting for transfers between devices: 15.3 us -> 7.92 us
  Pallas kernels: 22.5 us -> 21.2 us
    all_to_all x1 -> x2, blocking collectives: 17.9 us -> 34.9 us  [exchange(): lax.all_to_all(block, 'order', split_axis=0, concat_axis=0, tiled=True)]
    all_to_all x2 -> x1, starting transfers between devices: 17 us -> 7.21 us  [exchange(): lax.all_to_all(block, 'order', split_axis=0, concat_axis=0, tiled=True)]
    ppermute x2, waiting for transfers between devices: 7.37 us -> 0.01 us  [shift(): lax.ppermute(block, 'axial', [(i, (i + offset) % count) for i in range(co...]
    pallas_call x1, Pallas kernels: 3.77 us -> 2.39 us  [radial_slope(): call(slope_kernel, 'radial_slope', pltpu.HBM((R, rows), BF16), [HERE] * 7...]
    all_to_all x2 -> x1, waiting for transfers between devices: 7.91 us -> 7.91 us  [exchange(): lax.all_to_all(block, 'order', split_axis=0, concat_axis=0, tiled=True)]
  transfers between devices with their start and end apart: 4 -> 3, of which waited for: 3 -> 1; matrix products, arithmetic and copies ran while one was open for 0% -> 0% of each run, Pallas kernels for 18% -> 13%
where the time goes in v6:
time: 78.2 us; the launch traced here: 77.8 us
  blocking collectives  34.9 us (45%)
  Pallas kernels  21.2 us (27%)
  starting transfers between devices  13.7 us (18%)
  waiting for transfers between devices  7.92 us (10%)
    all_to_all x2, blocking collectives, exchange(): lax.all_to_all(block, 'order', split_axis=0, concat_axis=0, tiled=True)  34.9 us
    all_to_all x1, waiting for transfers between devices, exchange(): lax.all_to_all(block, 'order', split_axis=0, concat_axis=0, tiled=True)  7.91 us
    all_to_all x1, starting transfers between devices, exchange(): lax.all_to_all(block, 'order', split_axis=0, concat_axis=0, tiled=True)  7.21 us
    ppermute x2, starting transfers between devices, shift(): lax.ppermute(block, 'axial', [(i, (i + offset) % count) for i in range(co...  6.48 us
    pallas_call x1, Pallas kernels, physical_stage(): call(functools.partial(physical_kernel, groups, band, step, scale), 'phys...  5.4 us
    pallas_call x1, Pallas kernels, radial_raw(): call(raw_kernel, 'radial_raw', (pltpu.HBM((R, rows), BF16), jax.ShapeDtyp...  3.98 us
    pallas_call x1, Pallas kernels, azimuthal_table(): call(functools.partial(table_kernel, slots), 'azimuthal_table', pltpu.HBM...  3.51 us
    pallas_call x1, Pallas kernels, axial_stage(): call(functools.partial(axial_kernel, groups, band), 'axial_stage', jax.Sh...  2.76 us
  transfers between devices with their start and end apart: 3, of which 1 were waited for; matrix products, arithmetic and copies ran while one was open for 0% of the time, Pallas kernels for 13%

profile of v6, /device:TPU:1, one launch (start us, length us, event | category | flops | bytes accessed | tf_op | source)
XLA Modules:
  0.0 77.8 jit_solution(3081656923471863346)
XLA Ops:
  0.0 1.3 %stage.1.x_ref = bf16[384,1024]{1,0:T(8,128)(2,1)S(1)} custom-call(bf16[4,2,32,2,1024]{4,3,2,1,0:T(2,128)(2,1)} %x_far.1), custom_call_target="tpu_custom_call" | custom-call | tf_op jit(solution)/shard_map/stage/pallas_call | solution.py:85
  1.3 0.0 copy-start
  1.3 0.0 copy-start.3
  1.3 6.5 %collective-permute-start.1 = (bf16[384,1024]{1,0:T(8,128)(2,1)S(1)}, bf16[384,1024]{1,0:T(8,128)(2,1)S(1)}, u32[]{:S(2)}, u32[]{:S(2)}) collective-permute-start(bf16[384,1024]{1,0:T(8,128)(2,1)S(1)} %stage.1.x_ref), channel_id=1, source_target_pairs={{0,7},{1,0},{2,1},{3,2},{4,3},{5,4},{6,5},{7,6},{8,15},{9,8},{10,9... | collective-permute-start | bytes 2359304 | tf_op jit(solution)/shard_map/ppermute | solution.py:397
  7.8 0.0 collective-permute-start
  7.8 4.0 %radial_raw.1 = (bf16[1024,128]{1,0:T(8,128)(2,1)}, s32[128,128]{1,0:T(8,128)S(1)}, f32[128,128]{1,0:T(8,128)S(1)}) custom-call(s32[8,128]{1,0:T(8,128)} %bitcast.12, s32[8,128]{1,0:T(8,128)} %bitcast.16, bf16[4,2,32,2,1024]{4,3,2,1,0:T(2,128)(2,1)} %x_far.1, bf16[1024,1024]{1,0:T(8,128)(2,1)} %constant.8.clone.table_far.table_ref), custom_call_target="tpu_custom_call" | custom-call | tf_op jit(solution)/shard_map/radial_raw/pallas_call | solution.py:162
  11.8 17.0 %all_to_all.34 = bf16[32,32,128]{2,1,0:T(8,128)(2,1)S(1)} all-to-all(bf16[32,32,128]{2,1,0:T(8,128)(2,1)} %bitcast.15), channel_id=1, replica_groups=mesh['order'=32,'axial'=8] {'order'}, dimensions={0} | all-to-all | bytes 524288 | tf_op jit(solution)/shard_map/all_to_all | solution.py:401
  28.8 0.0 collective-permute-done.1.high_ref
  28.8 0.0 collective-permute-done.low_ref
  28.8 0.0 copy-done
  28.8 0.0 copy-done.3
  28.9 0.0 copy-start.4
  28.9 2.4 %radial_slope.1 = bf16[1024,384]{1,0:T(8,128)(2,1)} custom-call(bf16[384,1024]{1,0:T(8,128)(2,1)S(1)} %stage.1.x_ref, bf16[384,1024]{1,0:T(8,128)(2,1)S(1)} %collective-permute-done.low_ref, bf16[384,1024]{1,0:T(8,128)(2,1)S(1)} %collective-permute-done.1.high_ref, s32[128,128]{1,0:T(8,128)S(1)} %get-tuple-element.10.lens_ref, ...), custom_call_target="tpu_custom_call" | custom-call | tf_op jit(solution)/shard_map/radial_slope/pallas_call | solution.py:189
  31.3 7.2 %all-to-all-start.1 = ((bf16[32,32,384]{2,1,0:T(8,128)(2,1)}), bf16[32,32,384]{2,1,0:T(8,128)(2,1)S(1)}, u32[]{:S(2)}, u32[]{:S(2)}) async-start(bf16[32,32,384]{2,1,0:T(8,128)(2,1)} %bitcast.14), calls=%async_computation.1 | async-start | bytes 1572864 | tf_op jit(solution)/shard_map/all_to_all | solution.py:401
  38.5 0.0 copy-done.4
  38.5 0.0 copy-start.2
  38.5 3.5 %azimuthal_table.1.far_ref = bf16[1024,2176]{1,0:T(8,128)(2,1)} custom-call(s32[8,128]{1,0:T(8,128)S(1)} %bitcast.13), custom_call_target="tpu_custom_call" | custom-call | tf_op jit(solution)/shard_map/azimuthal_table/pallas_call | solution.py:239
  42.0 0.0 copy-done.2
  42.0 2.8 %axial_stage.1.axial_ref = f32[64,2176]{1,0:T(8,128)S(1)} custom-call(bf16[1024,128]{1,0:T(8,128)(2,1)S(1)} %bitcast.11, bf16[512,512]{1,0:T(8,128)(2,1)S(1)} %copy-done.2, bf16[1024,2176]{1,0:T(8,128)(2,1)} %azimuthal_table.1.far_ref), custom_call_target="tpu_custom_call" | custom-call | tf_op jit(solution)/shard_map/axial_stage/pallas_call | solution.py:297
  44.8 7.9 %all-to-all-done.1 = bf16[32,32,384]{2,1,0:T(8,128)(2,1)S(1)} async-done(((bf16[32,32,384]{2,1,0:T(8,128)(2,1)}), bf16[32,32,384]{2,1,0:T(8,128)(2,1)S(1)}, u32[]{:S(2)}, u32[]{:S(2)}) %all-to-all-start.1) | async-done | bytes 786464 | tf_op jit(solution)/shard_map/all_to_all | solution.py:401
  52.7 0.0 copy-start.1
  52.7 5.4 %physical_stage.1 = bf16[1024,384]{1,0:T(8,128)(2,1)S(1)} custom-call(bf16[1024,384]{1,0:T(8,128)(2,1)S(1)} %bitcast.8, f32[64,2176]{1,0:T(8,128)S(1)} %axial_stage.1.axial_ref, bf16[512,512]{1,0:T(8,128)(2,1)S(1)} %copy-done.2, bf16[1024,2176]{1,0:T(8,128)(2,1)} %azimuthal_table.1.far_ref), custom_call_target="tpu_custom_call" | custom-call | tf_op jit(solution)/shard_map/physical_stage/pallas_call | solution.py:362
  58.1 17.9 %all_to_all.35 = bf16[32,32,384]{2,1,0:T(8,128)(2,1)S(1)} all-to-all(bf16[32,32,384]{2,1,0:T(8,128)(2,1)S(1)} %bitcast.9), channel_id=1, replica_groups=mesh['order'=32,'axial'=8] {'order'}, dimensions={0} | all-to-all | bytes 1572864 | tf_op jit(solution)/shard_map/all_to_all | solution.py:401
  76.0 0.0 copy-done.1
  76.0 1.8 %radial_analysis.1 = bf16[3,2,32,2,1024]{4,3,2,1,0:T(2,128)(2,1)} custom-call(bf16[1024,384]{1,0:T(8,128)(2,1)S(1)} %bitcast.10, s32[128,128]{1,0:T(8,128)S(1)} %get-tuple-element.10.lens_ref, bf16[1024,1024]{1,0:T(8,128)(2,1)S(1)} %copy-done.1), custom_call_target="tpu_custom_call" | custom-call | tf_op jit(solution)/shard_map/radial_analysis/pallas_call | solution.py:389
Async XLA Ops:
  1.3 27.5 %copy-start = (bf16[1024,1024]{1,0:T(8,128)(2,1)S(1)}, bf16[1024,1024]{1,0:T(8,128)(2,1)}, u32[]{:S(2)}) copy-start(bf16[1024,1024]{1,0:T(8,128)(2,1)} %constant.8.clone.table_far.table_ref) | copy-start | bytes 6291460
  1.3 27.5 %copy-start.3 = (bf16[128,384]{1,0:T(8,128)(2,1)S(1)}, bf16[128,384]{1,0:T(8,128)(2,1)}, u32[]{:S(2)}) copy-start(bf16[128,384]{1,0:T(8,128)(2,1)} %constant.9.clone.rows_ref) | copy-start | bytes 294916
  1.3 27.5 %collective-permute-start.1 = (bf16[384,1024]{1,0:T(8,128)(2,1)S(1)}, bf16[384,1024]{1,0:T(8,128)(2,1)S(1)}, u32[]{:S(2)}, u32[]{:S(2)}) collective-permute-start(bf16[384,1024]{1,0:T(8,128)(2,1)S(1)} %stage.1.x_ref), channel_id=1, source_target_pairs={{0,7},{1,0},{2,1},{3,2},{4,3},{5,4},{6,5},{7,6},{8,15},{9,8},{10,9... | collective-permute-start | bytes 2359304 | tf_op jit(solution)/shard_map/ppermute | solution.py:397
  7.8 21.0 %collective-permute-start = (bf16[384,1024]{1,0:T(8,128)(2,1)S(1)}, bf16[384,1024]{1,0:T(8,128)(2,1)S(1)}, u32[]{:S(2)}, u32[]{:S(2)}) collective-permute-start(bf16[384,1024]{1,0:T(8,128)(2,1)S(1)} %stage.1.x_ref), channel_id=1, source_target_pairs={{0,1},{1,2},{2,3},{3,4},{4,5},{5,6},{6,7},{7,0},{8,9},{9,10},{10,1... | collective-permute-start | bytes 2359304 | tf_op jit(solution)/shard_map/ppermute | solution.py:397
  28.9 9.6 %copy-start.4 = (s32[1024]{0:T(1024)S(1)}, s32[1024]{0:T(1024)}, u32[]{:S(2)}) copy-start(s32[1024]{0:T(1024)} %param.8) | copy-start | bytes 12292
  31.3 21.4 %all-to-all-start.1 = ((bf16[32,32,384]{2,1,0:T(8,128)(2,1)}), bf16[32,32,384]{2,1,0:T(8,128)(2,1)S(1)}, u32[]{:S(2)}, u32[]{:S(2)}) async-start(bf16[32,32,384]{2,1,0:T(8,128)(2,1)} %bitcast.14), calls=%async_computation.1 | async-start | bytes 1572864 | tf_op jit(solution)/shard_map/all_to_all | solution.py:401
  38.5 3.5 %copy-start.2 = (bf16[512,512]{1,0:T(8,128)(2,1)S(1)}, bf16[512,512]{1,0:T(8,128)(2,1)}, u32[]{:S(2)}) copy-start(bf16[512,512]{1,0:T(8,128)(2,1)} %constant.10.clone.perm_ref) | copy-start | bytes 1572868
  52.7 23.3 %copy-start.1 = (bf16[1024,1024]{1,0:T(8,128)(2,1)S(1)}, bf16[1024,1024]{1,0:T(8,128)(2,1)}, u32[]{:S(2)}) copy-start(bf16[1024,1024]{1,0:T(8,128)(2,1)} %constant.11.clone.table_ref) | copy-start | bytes 6291460

commit v7 on v6

--- a/solution.py
+++ b/solution.py
@@ -129,21 +129,15 @@
     return jnp.concatenate([lens, lens], axis=0), jnp.concatenate([weight, weight], axis=0)
 
 
-def raw_kernel(orders_far, lengths_far, x_far, table_far, out_ref, lens_ref, weight_ref,
-               buffer, sem, orders, lengths, x_ref, small_sem, table, load_sem):
-    size = table.shape[0] // 4
+def raw_kernel(orders_far, lengths_far, x_far, table, out_ref, lens_ref, weight_ref,
+               buffer, sem, orders, lengths, x_ref, small_sem):
     small = [
         pltpu.make_async_copy(orders_far, orders, small_sem.at[0]),
         pltpu.make_async_copy(lengths_far, lengths, small_sem.at[1]),
         pltpu.make_async_copy(x_far.at[3, 0], x_ref.at[0], small_sem.at[2]),
         pltpu.make_async_copy(x_far.at[3, 1], x_ref.at[1], small_sem.at[3]),
     ]
-    loads = [
-        pltpu.make_async_copy(table_far.at[pl.ds(i * size, size)],
-                              table.at[pl.ds(i * size, size)], load_sem.at[i])
-        for i in range(4)
-    ]
-    for copy in small + loads:
+    for copy in small:
         copy.start()
     small[0].wait()
     small[1].wait()
@@ -154,7 +148,7 @@
     small[3].wait()
     block = x_ref[...]
     block = block.reshape(math.prod(block.shape[:-1]), block.shape[-1])
-    send_bands(table, masked_rows(block, lens, weight), out_ref, buffer, sem, loads)
+    send_bands(table, masked_rows(block, lens, weight), out_ref, buffer, sem)
 
 
 def radial_raw(orders, lengths, x, table):
@@ -164,12 +158,11 @@
         (pltpu.HBM((R, rows), BF16),
          jax.ShapeDtypeStruct((rows, 128), jnp.int32),
          jax.ShapeDtypeStruct((rows, 128), F32)),
-        [FAR] * 4, (FAR, HERE, HERE),
+        [FAR] * 3 + [HERE], (FAR, HERE, HERE),
         [pltpu.VMEM((R, rows), BF16), pltpu.SemaphoreType.DMA((4,)),
          pltpu.VMEM(orders.shape, jnp.int32), pltpu.VMEM(lengths.shape, jnp.int32),
-         pltpu.VMEM(x.shape[1:], BF16), pltpu.SemaphoreType.DMA((4,)),
-         pltpu.VMEM(table.shape, BF16), pltpu.SemaphoreType.DMA((4,))],
-    )(in_hbm(orders), in_hbm(lengths), in_hbm(x), in_hbm(table))
+         pltpu.VMEM(x.shape[1:], BF16), pltpu.SemaphoreType.DMA((4,))],
+    )(in_hbm(orders), in_hbm(lengths), in_hbm(x), table)
 
 
 def slope_kernel(x_ref, low_ref, high_ref, lens_ref, weight_ref, rows_ref, table_ref, out_ref,

time: 78.2 us -> 78.2 us (level)
  local copies, waits for them, and re-layouts: 0.03 us -> 1.62 us
  Pallas kernels: 21.2 us -> 20 us
    unnamed x10 -> x12, local copies, waits for them, and re-layouts: 0.03 us -> 1.62 us
    pallas_call x1, Pallas kernels: 3.98 us -> 2.79 us  [radial_raw(): call(raw_kernel, 'radial_raw', (pltpu.HBM((R, rows), BF16), jax.ShapeDtyp...]
  transfers between devices with their start and end apart: 3 -> 3, of which waited for: 1 -> 1; matrix products, arithmetic and copies ran while one was open for 0% -> 0% of each run, Pallas kernels for 13% -> 12%
where the time goes in v7:
time: 78.2 us; the launch traced here: 77.8 us
  blocking collectives  34.9 us (45%)
  Pallas kernels  20 us (26%)
  starting transfers between devices  13.3 us (17%)
  waiting for transfers between devices  7.92 us (10%)
  local copies, waits for them, and re-layouts  1.62 us (2%)
    all_to_all x2, blocking collectives, exchange(): lax.all_to_all(block, 'order', split_axis=0, concat_axis=0, tiled=True)  34.9 us
    all_to_all x1, waiting for transfers between devices, exchange(): lax.all_to_all(block, 'order', split_axis=0, concat_axis=0, tiled=True)  7.92 us
    all_to_all x1, starting transfers between devices, exchange(): lax.all_to_all(block, 'order', split_axis=0, concat_axis=0, tiled=True)  6.81 us
    ppermute x2, starting transfers between devices, shift(): lax.ppermute(block, 'axial', [(i, (i + offset) % count) for i in range(co...  6.48 us
    pallas_call x1, Pallas kernels, physical_stage(): call(functools.partial(physical_kernel, groups, band, step, scale), 'phys...  5.42 us
    pallas_call x1, Pallas kernels, azimuthal_table(): call(functools.partial(table_kernel, slots), 'azimuthal_table', pltpu.HBM...  3.5 us
    pallas_call x1, Pallas kernels, radial_raw(): call(raw_kernel, 'radial_raw', (pltpu.HBM((R, rows), BF16), jax.ShapeDtyp...  2.79 us
    pallas_call x1, Pallas kernels, axial_stage(): call(functools.partial(axial_kernel, groups, band), 'axial_stage', jax.Sh...  2.75 us
  transfers between devices with their start and end apart: 3, of which 1 were waited for; matrix products, arithmetic and copies ran while one was open for 0% of the time, Pallas kernels for 12%

profile of v7, /device:TPU:1, one launch (start us, length us, event | category | flops | bytes accessed | tf_op | source)
XLA Modules:
  0.0 77.8 jit_solution(5721945749341589542)
XLA Ops:
  0.0 0.0 copy-start.4
  0.0 1.3 %stage.1.x_ref = bf16[384,1024]{1,0:T(8,128)(2,1)S(1)} custom-call(bf16[4,2,32,2,1024]{4,3,2,1,0:T(2,128)(2,1)} %x_far.1), custom_call_target="tpu_custom_call" | custom-call | tf_op jit(solution)/shard_map/stage/pallas_call | solution.py:85
  1.3 6.5 %collective-permute-start.1 = (bf16[384,1024]{1,0:T(8,128)(2,1)S(1)}, bf16[384,1024]{1,0:T(8,128)(2,1)S(1)}, u32[]{:S(2)}, u32[]{:S(2)}) collective-permute-start(bf16[384,1024]{1,0:T(8,128)(2,1)S(1)} %stage.1.x_ref), channel_id=1, source_target_pairs={{0,7},{1,0},{2,1},{3,2},{4,3},{5,4},{6,5},{7,6},{8,15},{9,8},{10,9... | collective-permute-start | bytes 2359304 | tf_op jit(solution)/shard_map/ppermute | solution.py:390
  7.8 0.0 collective-permute-start
  7.8 0.0 copy-start
  7.8 1.6 %copy-done = bf16[1024,1024]{1,0:T(8,128)(2,1)S(1)} copy-done((bf16[1024,1024]{1,0:T(8,128)(2,1)S(1)}, bf16[1024,1024]{1,0:T(8,128)(2,1)}, u32[]{:S(2)}) %copy-start) | copy-done | bytes 2097176
  9.4 0.0 copy-start.1
  9.4 2.8 %radial_raw.1 = (bf16[1024,128]{1,0:T(8,128)(2,1)}, s32[128,128]{1,0:T(8,128)S(1)}, f32[128,128]{1,0:T(8,128)S(1)}) custom-call(s32[8,128]{1,0:T(8,128)} %bitcast.12, s32[8,128]{1,0:T(8,128)} %bitcast.16, bf16[4,2,32,2,1024]{4,3,2,1,0:T(2,128)(2,1)} %x_far.1, bf16[1024,1024]{1,0:T(8,128)(2,1)S(1)} %copy-done), custom_call_target="tpu_custom_call" | custom-call | tf_op jit(solution)/shard_map/radial_raw/pallas_call | solution.py:156
  12.2 17.0 %all_to_all.34 = bf16[32,32,128]{2,1,0:T(8,128)(2,1)S(1)} all-to-all(bf16[32,32,128]{2,1,0:T(8,128)(2,1)} %bitcast.15), channel_id=1, replica_groups=mesh['order'=32,'axial'=8] {'order'}, dimensions={0} | all-to-all | bytes 524288 | tf_op jit(solution)/shard_map/all_to_all | solution.py:394
  29.2 0.0 collective-permute-done.1.high_ref
  29.2 0.0 collective-permute-done.low_ref
  29.2 0.0 copy-done.4
  29.2 0.0 copy-done.1
  29.3 0.0 copy-start.5
  29.3 2.4 %radial_slope.1 = bf16[1024,384]{1,0:T(8,128)(2,1)} custom-call(bf16[384,1024]{1,0:T(8,128)(2,1)S(1)} %stage.1.x_ref, bf16[384,1024]{1,0:T(8,128)(2,1)S(1)} %collective-permute-done.low_ref, bf16[384,1024]{1,0:T(8,128)(2,1)S(1)} %collective-permute-done.1.high_ref, s32[128,128]{1,0:T(8,128)S(1)} %get-tuple-element.10.lens_ref, ...), custom_call_target="tpu_custom_call" | custom-call | tf_op jit(solution)/shard_map/radial_slope/pallas_call | solution.py:182
  31.7 6.8 %all-to-all-start.1 = ((bf16[32,32,384]{2,1,0:T(8,128)(2,1)}), bf16[32,32,384]{2,1,0:T(8,128)(2,1)S(1)}, u32[]{:S(2)}, u32[]{:S(2)}) async-start(bf16[32,32,384]{2,1,0:T(8,128)(2,1)} %bitcast.14), calls=%async_computation.1 | async-start | bytes 1572864 | tf_op jit(solution)/shard_map/all_to_all | solution.py:394
  38.5 0.0 copy-done.5
  38.5 0.0 copy-start.3
  38.5 3.5 %azimuthal_table.1.far_ref = bf16[1024,2176]{1,0:T(8,128)(2,1)} custom-call(s32[8,128]{1,0:T(8,128)S(1)} %bitcast.13), custom_call_target="tpu_custom_call" | custom-call | tf_op jit(solution)/shard_map/azimuthal_table/pallas_call | solution.py:232
  42.0 0.0 copy-done.3
  42.0 2.8 %axial_stage.1.axial_ref = f32[64,2176]{1,0:T(8,128)S(1)} custom-call(bf16[1024,128]{1,0:T(8,128)(2,1)S(1)} %bitcast.11, bf16[512,512]{1,0:T(8,128)(2,1)S(1)} %copy-done.3, bf16[1024,2176]{1,0:T(8,128)(2,1)} %azimuthal_table.1.far_ref), custom_call_target="tpu_custom_call" | custom-call | tf_op jit(solution)/shard_map/axial_stage/pallas_call | solution.py:290
  44.8 7.9 %all-to-all-done.1 = bf16[32,32,384]{2,1,0:T(8,128)(2,1)S(1)} async-done(((bf16[32,32,384]{2,1,0:T(8,128)(2,1)}), bf16[32,32,384]{2,1,0:T(8,128)(2,1)S(1)}, u32[]{:S(2)}, u32[]{:S(2)}) %all-to-all-start.1) | async-done | bytes 786464 | tf_op jit(solution)/shard_map/all_to_all | solution.py:394
  52.7 0.0 copy-start.2
  52.7 5.4 %physical_stage.1 = bf16[1024,384]{1,0:T(8,128)(2,1)S(1)} custom-call(bf16[1024,384]{1,0:T(8,128)(2,1)S(1)} %bitcast.8, f32[64,2176]{1,0:T(8,128)S(1)} %axial_stage.1.axial_ref, bf16[512,512]{1,0:T(8,128)(2,1)S(1)} %copy-done.3, bf16[1024,2176]{1,0:T(8,128)(2,1)} %azimuthal_table.1.far_ref), custom_call_target="tpu_custom_call" | custom-call | tf_op jit(solution)/shard_map/physical_stage/pallas_call | solution.py:355
  58.1 17.8 %all_to_all.35 = bf16[32,32,384]{2,1,0:T(8,128)(2,1)S(1)} all-to-all(bf16[32,32,384]{2,1,0:T(8,128)(2,1)S(1)} %bitcast.9), channel_id=1, replica_groups=mesh['order'=32,'axial'=8] {'order'}, dimensions={0} | all-to-all | bytes 1572864 | tf_op jit(solution)/shard_map/all_to_all | solution.py:394
  76.0 0.0 copy-done.2
  76.0 1.8 %radial_analysis.1 = bf16[3,2,32,2,1024]{4,3,2,1,0:T(2,128)(2,1)} custom-call(bf16[1024,384]{1,0:T(8,128)(2,1)S(1)} %bitcast.10, s32[128,128]{1,0:T(8,128)S(1)} %get-tuple-element.10.lens_ref, bf16[1024,1024]{1,0:T(8,128)(2,1)S(1)} %copy-done.2), custom_call_target="tpu_custom_call" | custom-call | tf_op jit(solution)/shard_map/radial_analysis/pallas_call | solution.py:382
Async XLA Ops:
  0.0 29.2 %copy-start.4 = (bf16[128,384]{1,0:T(8,128)(2,1)S(1)}, bf16[128,384]{1,0:T(8,128)(2,1)}, u32[]{:S(2)}) copy-start(bf16[128,384]{1,0:T(8,128)(2,1)} %constant.9.clone.rows_ref) | copy-start | bytes 294916
  1.3 27.9 %collective-permute-start.1 = (bf16[384,1024]{1,0:T(8,128)(2,1)S(1)}, bf16[384,1024]{1,0:T(8,128)(2,1)S(1)}, u32[]{:S(2)}, u32[]{:S(2)}) collective-permute-start(bf16[384,1024]{1,0:T(8,128)(2,1)S(1)} %stage.1.x_ref), channel_id=1, source_target_pairs={{0,7},{1,0},{2,1},{3,2},{4,3},{5,4},{6,5},{7,6},{8,15},{9,8},{10,9... | collective-permute-start | bytes 2359304 | tf_op jit(solution)/shard_map/ppermute | solution.py:390
  7.8 21.4 %collective-permute-start = (bf16[384,1024]{1,0:T(8,128)(2,1)S(1)}, bf16[384,1024]{1,0:T(8,128)(2,1)S(1)}, u32[]{:S(2)}, u32[]{:S(2)}) collective-permute-start(bf16[384,1024]{1,0:T(8,128)(2,1)S(1)} %stage.1.x_ref), channel_id=1, source_target_pairs={{0,1},{1,2},{2,3},{3,4},{4,5},{5,6},{6,7},{7,0},{8,9},{9,10},{10,1... | collective-permute-start | bytes 2359304 | tf_op jit(solution)/shard_map/ppermute | solution.py:390
  7.8 1.6 %copy-start = (bf16[1024,1024]{1,0:T(8,128)(2,1)S(1)}, bf16[1024,1024]{1,0:T(8,128)(2,1)}, u32[]{:S(2)}) copy-start(bf16[1024,1024]{1,0:T(8,128)(2,1)} %constant.8.clone.table.table_ref) | copy-start | bytes 6291460
  9.4 19.8 %copy-start.1 = (bf16[1024,1024]{1,0:T(8,128)(2,1)S(1)}, bf16[1024,1024]{1,0:T(8,128)(2,1)}, u32[]{:S(2)}) copy-start(bf16[1024,1024]{1,0:T(8,128)(2,1)} %constant.8.clone.table.table_ref) | copy-start | bytes 6291460
  29.3 9.2 %copy-start.5 = (s32[1024]{0:T(1024)S(1)}, s32[1024]{0:T(1024)}, u32[]{:S(2)}) copy-start(s32[1024]{0:T(1024)} %param.8) | copy-start | bytes 12292
  31.7 21.0 %all-to-all-start.1 = ((bf16[32,32,384]{2,1,0:T(8,128)(2,1)}), bf16[32,32,384]{2,1,0:T(8,128)(2,1)S(1)}, u32[]{:S(2)}, u32[]{:S(2)}) async-start(bf16[32,32,384]{2,1,0:T(8,128)(2,1)} %bitcast.14), calls=%async_computation.1 | async-start | bytes 1572864 | tf_op jit(solution)/shard_map/all_to_all | solution.py:394
  38.5 3.5 %copy-start.3 = (bf16[512,512]{1,0:T(8,128)(2,1)S(1)}, bf16[512,512]{1,0:T(8,128)(2,1)}, u32[]{:S(2)}) copy-start(bf16[512,512]{1,0:T(8,128)(2,1)} %constant.10.clone.perm_ref) | copy-start | bytes 1572868
  52.7 23.3 %copy-start.2 = (bf16[1024,1024]{1,0:T(8,128)(2,1)S(1)}, bf16[1024,1024]{1,0:T(8,128)(2,1)}, u32[]{:S(2)}) copy-start(bf16[1024,1024]{1,0:T(8,128)(2,1)} %constant.11.clone.table_ref) | copy-start | bytes 6291460
